TPU v7x, 256 devices: a whole 4x4x8 slice. The times are simulated.
256 devices in a mesh: lat: 16 (over x, y), mem: 16 (over z, core).
Axes of the slice: x: 4, y: 4, z: 8, core: 2. Of those that a mesh axis runs over, the one named last changes fastest.
Arguments:
- latent_field: bfloat16 [32, 16, 720, 256], P('mem', 'lat'), may hold values from -36 to 36
- norm_multipliers: float32 [2, 256], replicated, may hold values from 0.1 to 1.9
- kernel_coefficients: bfloat16 [2, 2304, 256], replicated, may hold values from -0.125 to 0.125
- expansion_matrix: bfloat16 [2, 256, 1024], replicated, may hold values from -0.375 to 0.375
- contraction_matrix: bfloat16 [2, 1024, 256], replicated, may hold values from -0.1875 to 0.1875
- obs_cell: int32 [16384], P('lat'), may hold values from 0 to 719
- obs_chan: int32 [16384], P('lat'), may hold values from 0 to 255
- obs_value: float32 [16384], P('lat'), may hold values from -16 to 16
- obs_var: float32 [16384], P('lat'), may hold values from 34.1333333 to 409.6
Outputs:
- posterior_latent: bfloat16 [32, 16, 720, 256], P('mem', 'lat')
Inputs may be any that keep to these rules, and one draw needn't show every extreme that they name: Observation i lies in latitude rows (i // 1024) * 1 onward; obs_cell[i] counts the cells of those 1 row row by row over 720 longitudes.
All inputs are finite; a program needn't handle non-finite values.
Results may differ from a plain program's by a relative error of at most 0.015.
Values may be sent and summed in bfloat16 or wider, within the bound.
No kernel may reach another device: no remote copies, remote signals or barrier semaphores. Data moves between devices by JAX's collectives and lax.ppermute only.
A program may use at most 192 MiB of HBM per device.

v0:
```python
import math

import jax
import jax.numpy as jnp
from jax import lax
from jax.sharding import PartitionSpec as P

BLOCKS = 2
NS_ITERS = 6


def padded_2(shard, sides, width):
    for axis, dim in sides:
        count, length = (lax.axis_size(axis), shard.shape[dim])
        up = [(i, (i + 1) % count) for i in range(count - 1)]
        down = [(j, i) for i, j in up]
        last = lax.slice_in_dim(shard, length - width, length, axis=dim)
        initial = lax.slice_in_dim(shard, 0, width, axis=dim)
        before = lax.ppermute(last, axis, up)
        after = lax.ppermute(initial, axis, down)
        shard = jnp.concatenate([before, shard, after], axis=dim)
    return shard


def normed(fields, gain):
    wide = fields.astype(jnp.float32)
    factor = lax.rsqrt(jnp.mean(wide * wide, axis=-1, keepdims=True) + 1e-06)
    return (wide * factor * gain).astype(jnp.bfloat16)


def columns(padded, height):
    pieces = []
    for lat_shift in range(3):
        lat_band = padded[:, lat_shift : lat_shift + height]
        for lon_shift in (-1, 0, 1):
            pieces.append(jnp.roll(lat_band, -lon_shift, axis=2))
    return jnp.concatenate(pieces, axis=-1)


def mix_layer(fields, padded, conv_mat, up_mat, down_mat):
    stacked = columns(padded, fields.shape[1])
    flat_cols = stacked.reshape(-1, stacked.shape[-1])
    conv_out = jnp.dot(flat_cols, conv_mat, preferred_element_type=jnp.float32).astype(jnp.bfloat16)
    hidden = jax.nn.gelu(jnp.dot(conv_out, up_mat, preferred_element_type=jnp.float32)).astype(
        jnp.bfloat16
    )
    branch = jnp.dot(hidden, down_mat, preferred_element_type=jnp.float32)
    return (fields.astype(jnp.float32) + branch.reshape(fields.shape)).astype(jnp.bfloat16)


def gram_terms(measured_entries, obs_value, obs_var):
    centre = jnp.mean(measured_entries, axis=0)
    anomaly = measured_entries - centre
    scaled = anomaly / obs_var
    gram_part = jnp.dot(scaled, anomaly.T, precision=lax.Precision.HIGHEST)
    drive_part = jnp.dot(scaled, obs_value - centre, precision=lax.Precision.HIGHEST)
    return (gram_part, drive_part)


def transform(gram_sum, drive_sum):
    realization_latents = gram_sum.shape[0]
    identity = jnp.eye(realization_latents, dtype=jnp.float32)
    spread = float(realization_latents - 1)
    system = spread * identity + gram_sum
    bound_value = spread + jnp.trace(gram_sum)
    iterate = system / bound_value
    inv_root = identity
    for sweep in range(NS_ITERS):
        step_mat = 1.5 * identity - 0.5 * jnp.dot(
            inv_root, iterate, precision=lax.Precision.HIGHEST
        )
        iterate = jnp.dot(iterate, step_mat, precision=lax.Precision.HIGHEST)
        inv_root = jnp.dot(step_mat, inv_root, precision=lax.Precision.HIGHEST)
    inv_sqrt = inv_root / jnp.sqrt(bound_value)
    mean_shift = jnp.dot(
        inv_sqrt,
        jnp.dot(inv_sqrt, drive_sum, precision=lax.Precision.HIGHEST),
        precision=lax.Precision.HIGHEST,
    )
    weights = math.sqrt(spread) * inv_sqrt + mean_shift[:, None]
    totals = jnp.sum(weights, axis=0)
    return (weights + (1.0 - totals)[None, :] / realization_latents).astype(jnp.bfloat16)


def body(
    latent_field,
    norm_multipliers,
    kernel_coefficients,
    expansion_matrix,
    contraction_matrix,
    obs_cell,
    obs_chan,
    obs_value,
    obs_var,
):
    fields = latent_field
    for layer_index in range(BLOCKS):
        unit = normed(fields, norm_multipliers[layer_index])
        padded = padded_2(unit, (("lat", 1),), 1)
        fields = mix_layer(
            fields,
            padded,
            kernel_coefficients[layer_index],
            expansion_matrix[layer_index],
            contraction_matrix[layer_index],
        )
    local_members = fields.shape[0]
    channels = fields.shape[3]
    linear_position = obs_cell * channels + obs_chan
    measured_entries = jnp.take(fields.reshape(local_members, -1), linear_position, axis=1)
    every_obs = lax.all_gather(measured_entries, "mem", axis=0, tiled=True).astype(jnp.float32)
    gram_part, drive_part = gram_terms(every_obs, obs_value, obs_var)
    gram_sum, drive_sum = lax.psum((gram_part, drive_part), "lat")
    square_array = transform(gram_sum, drive_sum)
    my_start = lax.axis_index("mem") * local_members
    my_cols = lax.dynamic_slice_in_dim(square_array, my_start, local_members, 1)
    initial = jnp.zeros(fields.shape, jnp.float32)
    piece = lax.all_gather(fields, "mem", axis=0, tiled=True)
    weight_rows = lax.slice_in_dim(my_cols, 0, piece.shape[0], axis=0)
    return (
        initial
        + jnp.einsum("kj,klnc->jlnc", weight_rows, piece, preferred_element_type=jnp.float32)
    ).astype(jnp.bfloat16)


def solution(mesh):
    in_specs = (
        P("mem", "lat", None, None),
        P(),
        P(),
        P(),
        P(),
        P("lat"),
        P("lat"),
        P("lat"),
        P("lat"),
    )
    out_specs = P("mem", "lat", None, None)
    return jax.shard_map(body, mesh=mesh, in_specs=in_specs, out_specs=out_specs, check_vma=False)
```

profile of v0, /device:TPU:0, one launch (start us, length us, event | category | flops | bytes accessed | tf_op | source)
XLA Modules:
  0.0 241.8 jit_solution(8468085395368767395)
XLA Ops:
  6.5 0.8 fusion.87
  7.3 1.4 fusion.19
  8.7 1.4 fusion.21
  10.1 1.8 collective-permute-start
  11.9 1.3 collective-permute-start.1
  13.2 0.2 fusion.83
  13.4 14.1 %collective-permute-done = bf16[2,1,720,256]{3,2,0,1:T(8,128)(2,1)S(1)} collective-permute-done((bf16[2,1,720,256]{3,2,0,1:T(8,128)(2,1)S(1)}, bf16[2,1,720,256]{3,2,0,1:T(8,128)(2,1)S(1)}, u32[]{:S(2)}, u32[]{:S(2)}) %collective-permute-start) | collective-permute-done | bytes 737312 | tf_op jit(solution)/shard_map/ppermute | solution.py:19
  27.6 0.2 fusion.85
  27.8 0.2 maximum_dynamic-update-slice_fusion.5
  28.1 0.2 maximum_dynamic-update-slice_fusion.3
  28.3 0.3 constant_dynamic-update-slice_fusion.1
  28.7 3.1 %collective-permute-done.1 = bf16[2,1,720,256]{3,2,0,1:T(8,128)(2,1)S(1)} collective-permute-done((bf16[2,1,720,256]{3,2,0,1:T(8,128)(2,1)S(1)}, bf16[2,1,720,256]{3,2,0,1:T(8,128)(2,1)S(1)}, u32[]{:S(2)}, u32[]{:S(2)}) %collective-permute-start.1) | collective-permute-done | bytes 737312 | tf_op jit(solution)/shard_map/ppermute | solution.py:20
  31.7 0.2 fusion.81
  32.0 0.2 maximum_dynamic-update-slice_fusion.1
  32.3 2.7 %copy-done.1 = bf16[2,1,720,2304]{3,2,0,1:T(8,128)(2,1)} copy-done((bf16[2,1,720,2304]{3,2,0,1:T(8,128)(2,1)}, bf16[2,1,720,2304]{3,2,0,1:T(8,128)(2,1)S(1)}, u32[]{:S(2)}) %copy-start.1) | copy-done | bytes 6635544
  35.0 9.1 %fusion.10 = bf16[1440,1024]{1,0:T(8,128)(2,1)} fusion(bf16[1440,2304]{1,0:T(8,128)(2,1)} %bitcast.109, bf16[2,2304,256]{2,1,0:T(8,128)(2,1)} %param.11, bf16[2,256,1024]{2,1,0:T(8,128)(2,1)S(1)} %copy-done.6), kind=kOutput, calls=%fused_computation.13 | convolution fusion | flops 2467307520 | bytes 11288576 | tf_op jit(solution)/shard_map/dot_general | solution.py:44
  44.1 3.0 %fusion.23 = (f32[2,720]{1,0:T(2,128)S(1)}, bf16[2,1,720,256]{3,2,0,1:T(8,128)(2,1)S(1)}) fusion(bf16[2,720,1024]{2,1,0:T(8,128)(2,1)} %bitcast.116, bf16[2,1024,256]{2,1,0:T(8,128)(2,1)} %param.13, bf16[2,1,720,256]{3,2,1,0:T(8,128)(2,1)S(1)} %copy-done), kind=kOutput, calls=%fused_computation.34 | convolution fusion | flops 757185152 | bytes 4953728 | tf_op jit(solution)/shard_map/dot_general | solution.py:47
  47.1 0.3 fusion.25
  47.4 3.5 %collective-permute-start.2 = (bf16[2,1,720,256]{3,2,0,1:T(8,128)(2,1)S(1)}, bf16[2,1,720,256]{3,2,0,1:T(8,128)(2,1)S(1)}, u32[]{:S(2)}, u32[]{:S(2)}) collective-permute-start(bf16[2,1,720,256]{3,2,0,1:T(8,128)(2,1)S(1)} %fusion.25), channel_id=1, source_target_pairs={{0,16},{16,32},{32,48},{48,64},{64,80},{80,96},{96,112},{112,128},... | collective-permute-start | bytes 2211848 | tf_op jit(solution)/shard_map/ppermute | solution.py:19
  50.9 1.5 collective-permute-start.3
  52.4 0.2 fusion.77
  52.6 12.8 %collective-permute-done.2 = bf16[2,1,720,256]{3,2,0,1:T(8,128)(2,1)S(1)} collective-permute-done((bf16[2,1,720,256]{3,2,0,1:T(8,128)(2,1)S(1)}, bf16[2,1,720,256]{3,2,0,1:T(8,128)(2,1)S(1)}, u32[]{:S(2)}, u32[]{:S(2)}) %collective-permute-start.2) | collective-permute-done | bytes 737312 | tf_op jit(solution)/shard_map/ppermute | solution.py:19
  65.4 0.2 fusion.79
  65.6 0.2 maximum_dynamic-update-slice_fusion.11
  65.9 0.2 maximum_dynamic-update-slice_fusion.9
  66.1 0.3 constant_dynamic-update-slice_fusion.4
  66.4 3.1 %collective-permute-done.3 = bf16[2,1,720,256]{3,2,0,1:T(8,128)(2,1)S(1)} collective-permute-done((bf16[2,1,720,256]{3,2,0,1:T(8,128)(2,1)S(1)}, bf16[2,1,720,256]{3,2,0,1:T(8,128)(2,1)S(1)}, u32[]{:S(2)}, u32[]{:S(2)}) %collective-permute-start.3) | collective-permute-done | bytes 737312 | tf_op jit(solution)/shard_map/ppermute | solution.py:20
  69.5 0.2 fusion.75
  69.8 0.2 maximum_dynamic-update-slice_fusion.7
  70.1 2.7 %copy-done.2 = bf16[2,1,720,2304]{3,2,0,1:T(8,128)(2,1)} copy-done((bf16[2,1,720,2304]{3,2,0,1:T(8,128)(2,1)}, bf16[2,1,720,2304]{3,2,0,1:T(8,128)(2,1)S(1)}, u32[]{:S(2)}) %copy-start.2) | copy-done | bytes 6635544
  72.8 9.1 %fusion.18 = bf16[1440,1024]{1,0:T(8,128)(2,1)} fusion(bf16[1440,2304]{1,0:T(8,128)(2,1)} %bitcast.110, bf16[2,2304,256]{2,1,0:T(8,128)(2,1)} %param.11, bf16[2,256,1024]{2,1,0:T(8,128)(2,1)S(1)} %copy-done.6), kind=kOutput, calls=%fused_computation.21 | convolution fusion | flops 2467307520 | bytes 11288576 | tf_op jit(solution)/shard_map/dot_general | solution.py:44
  81.9 3.8 %fusion.26 = bf16[2,1,720,256]{3,2,0,1:T(8,128)(2,1)} fusion(bf16[2,1,720,256]{3,2,0,1:T(8,128)(2,1)S(1)} %get-tuple-element.38, bf16[2,720,1024]{2,1,0:T(8,128)(2,1)} %bitcast.117, bf16[2,1024,256]{2,1,0:T(8,128)(2,1)} %param.13), kind=kOutput, calls=%fused_computation.37 | convolution fusion | flops 756080640 | bytes 4947968 | tf_op jit(solution)/shard_map/dot_general | solution.py:47
  85.8 31.0 %copy.25 = bf16[2,1,720,256]{0,3,2,1:T(8,128)(2,1)} copy(bf16[2,1,720,256]{3,2,0,1:T(8,128)(2,1)} %fusion.26) | data formatting | bytes 1474560 | tf_op jit(solution)/shard_map/reshape | solution.py:110
  116.7 11.3 %gather_fusion = bf16[1024,2]{1,0:T(8,128)(2,1)S(1)} fusion(bf16[2,184320]{0,1:T(8,128)(2,1)} %bitcast.107, s32[1024]{0:T(1024)S(1)} %broadcast_clamp_fusion), kind=kCustom, calls=%fused_computation | custom fusion | bytes 12288 | tf_op jit(solution)/shard_map/jit(_take)/gather | solution.py:110
  128.0 0.2 select_bitcast_fusion
  128.3 0.1 copy.21
  128.4 20.4 %all-gather = bf16[16,2,1024]{2,1,0:T(2,128)(2,1)S(1)} all-gather(bf16[1,2,1024]{2,1,0:T(2,128)(2,1)S(1)} %copy.21), channel_id=1, replica_groups=mesh['lat'=16,'mem'=16] {'mem'}, dimensions={0}, use_global_device_ids=true | all-gather | bytes 69632 | tf_op jit(solution)/shard_map/all_gather | solution.py:111
  148.9 0.2 convolution_bitcast_fusion.2
  149.1 0.3 fusion.55
  149.4 72.1 %all-reduce = (f32[32,32]{1,0:T(8,128)S(1)}, f32[32]{0:T(128)S(1)}) all-reduce(f32[32,32]{1,0:T(8,128)S(1)} %fusion.55, f32[32]{0:T(128)S(1)} %convolution_bitcast_fusion.2), channel_id=1, replica_groups=mesh['lat'=16,'mem'=16] {'lat'}, use_global_device_ids=true, to_apply=%region_3.4 | all-reduce | flops 1056 | bytes 8448 | tf_op jit(solution)/shard_map/psum | solution.py:113
  221.5 0.6 select_reduce_fusion
  222.8 0.1 fusion.46
  223.0 0.1 fusion.61
  223.1 0.1 fusion.62
  223.2 0.2 fusion.45
  223.4 0.1 fusion.89
  223.5 0.1 fusion.88
  223.7 0.2 fusion.44
  223.9 0.1 fusion.91
  224.0 0.1 fusion.90
  224.2 0.2 fusion.43
  224.3 0.1 fusion.93
  224.5 0.1 fusion.92
  224.6 0.2 fusion.42
  224.8 0.1 fusion.95
  224.9 0.1 fusion.94
  225.1 0.2 fusion.41
  225.2 0.2 convolution_divide_fusion
  225.5 0.1 convolution_bitcast_fusion.1
  225.6 0.1 convolution_bitcast_fusion
  225.7 0.1 fusion.74
  225.9 0.1 dynamic-slice
  226.0 8.0 %fusion.30 = bf16[2,1,720,256]{3,0,2,1:T(2,128)(2,1)S(1)} fusion(bf16[32,1,720,256]{3,2,1,0:T(8,128)(2,1)} %all-gather.3.cloned.1.call-done, f32[32,32]{0,1:T(8,128)S(1)} %get-tuple-element.8, s32[]{:T(128)S(6)} %select_n.20, f32[2]{0:T(128)S(1)} %dynamic-slice), kind=kOutput, calls=%fused_computation.39 | convolution fusion | flops 23961728 | bytes 12535300 | tf_op jit(solution)/shard_map/kj,klnc->jlnc/dot_general | solution.py:122
  234.0 1.0 copy.24
  (41 shorter events, 0.8 us)
Async XLA Ops:
  6.5 219.4 %all-gather.3.cloned.1.call-start = ((), (), s32[]{:S(2)}) async-start(), calls=%async_computation | async-start | bytes 12533760 | tf_op jit(solution)/shard_map/all_gather | solution.py:118
  10.1 17.5 %collective-permute-start = (bf16[2,1,720,256]{3,2,0,1:T(8,128)(2,1)S(1)}, bf16[2,1,720,256]{3,2,0,1:T(8,128)(2,1)S(1)}, u32[]{:S(2)}, u32[]{:S(2)}) collective-permute-start(bf16[2,1,720,256]{3,2,0,1:T(8,128)(2,1)S(1)} %fusion.21), channel_id=1, source_target_pairs={{0,16},{16,32},{32,48},{48,64},{64,80},{80,96},{96,112},{112,128},... | collective-permute-start | bytes 2211848 | tf_op jit(solution)/shard_map/ppermute | solution.py:19
  11.9 19.8 %collective-permute-start.1 = (bf16[2,1,720,256]{3,2,0,1:T(8,128)(2,1)S(1)}, bf16[2,1,720,256]{3,2,0,1:T(8,128)(2,1)S(1)}, u32[]{:S(2)}, u32[]{:S(2)}) collective-permute-start(bf16[2,1,720,256]{3,2,0,1:T(8,128)(2,1)S(1)} %fusion.21), channel_id=1, source_target_pairs={{16,0},{32,16},{48,32},{64,48},{80,64},{96,80},{112,96},{128,112},... | collective-permute-start | bytes 2211848 | tf_op jit(solution)/shard_map/ppermute | solution.py:20
  13.2 15.1 %copy-start = (bf16[2,1,720,256]{3,2,1,0:T(8,128)(2,1)S(1)}, bf16[2,1,720,256]{3,2,1,0:T(8,128)(2,1)}, u32[]{:S(2)}) copy-start(bf16[2,1,720,256]{3,2,1,0:T(8,128)(2,1)} %param.9) | copy-start | bytes 2211844
  28.1 6.9 %copy-start.6 = (bf16[2,256,1024]{2,1,0:T(8,128)(2,1)S(1)}, bf16[2,256,1024]{2,1,0:T(8,128)(2,1)}, u32[]{:S(2)}) copy-start(bf16[2,256,1024]{2,1,0:T(8,128)(2,1)} %param.12) | copy-start | bytes 3145732
  32.3 2.7 %copy-start.1 = (bf16[2,1,720,2304]{3,2,0,1:T(8,128)(2,1)}, bf16[2,1,720,2304]{3,2,0,1:T(8,128)(2,1)S(1)}, u32[]{:S(2)}) copy-start(bf16[2,1,720,2304]{3,2,0,1:T(8,128)(2,1)S(1)} %maximum_dynamic-update-slice_fusion) | copy-start | bytes 19906564
  47.4 18.0 %collective-permute-start.2 = (bf16[2,1,720,256]{3,2,0,1:T(8,128)(2,1)S(1)}, bf16[2,1,720,256]{3,2,0,1:T(8,128)(2,1)S(1)}, u32[]{:S(2)}, u32[]{:S(2)}) collective-permute-start(bf16[2,1,720,256]{3,2,0,1:T(8,128)(2,1)S(1)} %fusion.25), channel_id=1, source_target_pairs={{0,16},{16,32},{32,48},{48,64},{64,80},{80,96},{96,112},{112,128},... | collective-permute-start | bytes 2211848 | tf_op jit(solution)/shard_map/ppermute | solution.py:19
  50.9 18.6 %collective-permute-start.3 = (bf16[2,1,720,256]{3,2,0,1:T(8,128)(2,1)S(1)}, bf16[2,1,720,256]{3,2,0,1:T(8,128)(2,1)S(1)}, u32[]{:S(2)}, u32[]{:S(2)}) collective-permute-start(bf16[2,1,720,256]{3,2,0,1:T(8,128)(2,1)S(1)} %fusion.25), channel_id=1, source_target_pairs={{16,0},{32,16},{48,32},{64,48},{80,64},{96,80},{112,96},{128,112},... | collective-permute-start | bytes 2211848 | tf_op jit(solution)/shard_map/ppermute | solution.py:20
  70.1 2.7 %copy-start.2 = (bf16[2,1,720,2304]{3,2,0,1:T(8,128)(2,1)}, bf16[2,1,720,2304]{3,2,0,1:T(8,128)(2,1)S(1)}, u32[]{:S(2)}) copy-start(bf16[2,1,720,2304]{3,2,0,1:T(8,128)(2,1)S(1)} %maximum_dynamic-update-slice_fusion.6) | copy-start | bytes 19906564
  81.9 3.8 %copy-start.3 = (s32[1024]{0:T(1024)S(1)}, s32[1024]{0:T(1024)}, u32[]{:S(2)}) copy-start(s32[1024]{0:T(1024)} %param.15) | copy-start | bytes 12292
  81.9 3.8 %copy-start.4 = (s32[1024]{0:T(1024)S(1)}, s32[1024]{0:T(1024)}, u32[]{:S(2)}) copy-start(s32[1024]{0:T(1024)} %param.14) | copy-start | bytes 12292
  85.7 63.1 %copy-start.5 = (f32[1024]{0:T(1024)S(1)}, f32[1024]{0:T(1024)}, u32[]{:S(2)}) copy-start(f32[1024]{0:T(1024)} %param.16) | copy-start | bytes 12292
  85.8 63.1 %copy-start.7 = (f32[1024]{0:T(1024)S(1)}, f32[1024]{0:T(1024)}, u32[]{:S(2)}) copy-start(f32[1024]{0:T(1024)} %param.17) | copy-start | bytes 12292
Sparse Core Ops, SparseCore 0:
  85.8 77.2 all-gather.2
where the time goes:
time: 244 us; the launch traced here: 242 us
  blocking collectives  92.5 us (38%)
  local copies, waits for them, and re-layouts  51.2 us (21%)
  matrix products  36.3 us (15%)
  waiting for transfers between devices  33.1 us (14%)
  between operations  14.5 us (6%)
  starting transfers between devices  8.05 us (3%)
  other arithmetic  6.05 us (2%)
    psum x1, blocking collectives, body(): gram_sum, drive_sum = lax.psum((gram_part, drive_part), 'lat')  72.1 us
    reshape x1, local copies, waits for them, and re-layouts, body(): fields.reshape(local_members, -1)  31 us
    ppermute x2, waiting for transfers between devices, padded_2(): before = lax.ppermute(last, axis, up)  26.9 us
    all_gather x1, blocking collectives, body(): lax.all_gather(measured_entries, 'mem', axis=0, tiled=True)  20.4 us
    dot_general x2, matrix products, mix_layer(): jnp.dot(conv_out, up_mat, preferred_element_type=jnp.float32)  18.2 us
    gather x1, local copies, waits for them, and re-layouts, body(): jnp.take(fields.reshape(local_members, -1), linear_position, axis=1)  11.3 us
    dot_general x1, matrix products, body(): jnp.einsum('kj,klnc->jlnc', weight_rows, piece, preferred_element_type=jn...  8.04 us
    dot_general x2, matrix products, mix_layer(): branch = jnp.dot(hidden, down_mat, preferred_element_type=jnp.float32)  6.75 us
  transfers between devices with their start and end apart: 5, of which 4 were waited for; matrix products, arithmetic and copies ran while one was open for 20% of the time, Pallas kernels for 0%

commit v1 on v0

v1 whole, which is shorter than its diff:
```python
import functools
import math

import jax
import jax.numpy as jnp
from jax import lax
from jax.experimental import pallas as pl
from jax.experimental.pallas import tpu as pltpu
from jax.sharding import PartitionSpec as P

BLOCKS = 2
NS_ITERS = 6
F32 = jnp.float32
BF16 = jnp.bfloat16
HIGHEST = lax.Precision.HIGHEST
VMEM = pl.BlockSpec(memory_space=pltpu.VMEM)
SMEM = pl.BlockSpec(memory_space=pltpu.SMEM)
HBM = pl.BlockSpec(memory_space=pltpu.HBM)


def call(body, out_shape, args, specs=None, out_specs=None, scratch=(), mib=24, flops=0, nbytes=0, **kw):
    return pl.pallas_call(
        body,
        out_shape=out_shape,
        in_specs=specs or [VMEM] * len(args),
        out_specs=out_specs if out_specs is not None else jax.tree.map(lambda _: VMEM, out_shape),
        scratch_shapes=list(scratch),
        compiler_params=pltpu.CompilerParams(vmem_limit_bytes=mib << 20),
        cost_estimate=pl.CostEstimate(flops=flops, bytes_accessed=nbytes, transcendentals=0),
        **kw,
    )(*args)


def shaped(shape, dtype):
    return jax.ShapeDtypeStruct(shape, dtype)


def normed(wide, gain):
    factor = lax.rsqrt(jnp.mean(wide * wide, axis=-1, keepdims=True) + 1e-06)
    return (wide * factor * gain).astype(BF16)


def first_norm(x_ref, gain_ref, *unit_refs):
    for m, ref in enumerate(unit_refs):
        ref[...] = normed(x_ref[m, 0].astype(F32), gain_ref[0:1, :])


def load_body(*refs):
    sems, refs = refs[-1], refs[:-1]
    count = len(refs) // 2
    copies = []
    for ref, into in zip(refs[:count], refs[count:]):
        rows = ref.shape[1] // 4
        for b in range(ref.shape[0]):
            for i in range(4):
                part = pl.ds(i * rows, rows)
                copies.append(
                    pltpu.make_async_copy(ref.at[b, part], into.at[b, part], sems.at[len(copies)])
                )
    for copy in copies:
        copy.start()
    for copy in copies:
        copy.wait()


def block_body(b, member, odd_ref, x_ref, near_ref, mid_ref, far_ref, conv_ref, up_ref, down_ref, *rest):
    last = b == BLOCKS - 1
    *rest, mixed = rest
    if last and member == 0:
        cell_ref, chan_ref, out_ref, seen_ref, fields_ref = rest
    elif last:
        cell_ref, chan_ref, seen_ref, out_ref, fields_ref = rest
    elif member == 0:
        gain_ref, later_ref, fields_ref, pair_ref = rest
        unit_ref = pair_ref.at[0]
        pair_ref[1] = later_ref[...]
    else:
        gain_ref, fields_ref, unit_ref = rest
    lon, ch = x_ref.shape
    rows = jnp.concatenate([near_ref[...], mid_ref[...], far_ref[...]], axis=1)
    lines = (2 - 2 * odd_ref[0], 1, 2 * odd_ref[0])
    parts = []
    for q in range(3):
        taps = [
            conv_ref[b, pl.ds(pl.multiple_of((p * 3 + q) * ch, ch), ch), :] for p in lines
        ]
        parts.append(jnp.dot(rows, jnp.concatenate(taps, axis=0), preferred_element_type=F32))
    mixed[...] = (
        pltpu.roll(parts[0], 1, 0) + parts[1] + pltpu.roll(parts[2], lon - 1, 0)
    ).astype(BF16)
    step = 144
    for start in range(0, lon, step):
        part = pl.ds(start, step)
        hidden = jax.nn.gelu(jnp.dot(mixed[part, :], up_ref[b], preferred_element_type=F32))
        branch = jnp.dot(hidden.astype(BF16), down_ref[b], preferred_element_type=F32)
        fields = (x_ref[part, :].astype(F32) + branch).astype(BF16)
        fields_ref[part, :] = fields
        if not last:
            unit_ref[part, :] = normed(fields.astype(F32), gain_ref[b + 1 : b + 2, :])
    if last:
        owners = out_ref.shape[0]
        cells = fields_ref.shape[0] // owners
        count = cell_ref.shape[1]
        at_cell = lax.broadcasted_iota(jnp.int32, (lon, count), 0) == cell_ref[...]
        pick = jnp.where(at_cell, 1.0, 0.0).astype(BF16)
        column = lax.dot_general(
            fields_ref[:lon, :], pick, (((0,), (0,)), ((), ())), preferred_element_type=F32
        )
        at_chan = lax.broadcasted_iota(jnp.int32, (ch, count), 0) == chan_ref[...]
        seen = jnp.sum(jnp.where(at_chan, column, 0.0), axis=0, keepdims=True)
        seen = [seen[:, i : i + ch] for i in range(0, count, ch)]
        fields_ref[lon:, :] = jnp.zeros((owners * cells - lon, ch), BF16)
        for i in range(owners):
            out_ref[i, :cells, :] = fields_ref[i * cells : (i + 1) * cells, :]
        if member == 0:
            seen_ref[...] = jnp.concatenate(seen, axis=0)
        else:
            both = jnp.concatenate([seen_ref[...], *seen], axis=0).astype(BF16)
            for i in range(owners):
                out_ref[i, cells:, :] = both


def gram_body(seen_ref, value_ref, var_ref, out_ref):
    owners, _, ch = seen_ref.shape
    lines = value_ref.shape[0]
    seen = seen_ref[...].astype(F32)
    members = 2 * owners
    twice = lambda ref: jnp.concatenate([ref[...], ref[...]], axis=0)
    half = jnp.sum(seen, axis=0)
    centre = (half + pltpu.roll(half, lines, 0)) / members
    anomaly = seen - centre[None]
    scaled = anomaly / twice(var_ref)[None]
    rows = owners * 8
    right = jnp.concatenate([anomaly.reshape(rows, ch), twice(value_ref) - centre], axis=0)
    terms = lax.dot_general(
        scaled.reshape(rows, ch),
        right,
        (((1,), (1,)), ((), ())),
        precision=HIGHEST,
        preferred_element_type=F32,
    )
    row = lax.broadcasted_iota(jnp.int32, terms.shape, 0)
    col = lax.broadcasted_iota(jnp.int32, terms.shape, 1)
    terms = jnp.where((row % lines == col % lines) & (col < rows + lines), terms, 0.0)
    dot = functools.partial(jnp.dot, precision=HIGHEST, preferred_element_type=F32)
    left = jnp.where(
        lax.broadcasted_iota(jnp.int32, (members, rows), 0)
        == lax.broadcasted_iota(jnp.int32, (members, rows), 1) // lines,
        1.0,
        0.0,
    )
    gather = jnp.where(
        lax.broadcasted_iota(jnp.int32, (rows + 8, 128), 0) // lines
        == lax.broadcasted_iota(jnp.int32, (rows + 8, 128), 1),
        1.0,
        0.0,
    )
    out_ref[...] = dot(dot(left, terms), gather)


def transform_body(a_ref, b_ref, c_ref, d_ref, out_ref):
    total = (a_ref[...] + b_ref[...]) + (c_ref[...] + d_ref[...])
    members = total.shape[0]
    dot = functools.partial(jnp.dot, precision=HIGHEST, preferred_element_type=F32)
    row = lax.broadcasted_iota(jnp.int32, (members, members), 0)
    col = lax.broadcasted_iota(jnp.int32, (members, members), 1)
    identity = jnp.where(row == col, 1.0, 0.0)
    spread = float(members - 1)
    gram = total[:, :members]
    bound_value = spread + jnp.sum(gram * identity)
    iterate = (spread * identity + gram) / bound_value
    inv_root = identity
    for _ in range(NS_ITERS):
        step_mat = 1.5 * identity - 0.5 * dot(inv_root, iterate)
        iterate = dot(iterate, step_mat)
        inv_root = dot(step_mat, inv_root)
    inv_sqrt = inv_root / jnp.sqrt(bound_value)
    shift = dot(inv_sqrt, dot(inv_sqrt, total))[:, members : members + 1]
    weights = math.sqrt(spread) * inv_sqrt + shift
    totals = jnp.sum(weights, axis=0, keepdims=True)
    out_ref[...] = (weights + (1.0 - totals) / members).astype(BF16)


def combine_body(weight_ref, even_ref, odd_ref, out_ref):
    members = weight_ref.shape[0]
    owners = even_ref.shape[0]
    cells = out_ref.shape[1]
    group = 16
    rows = members * group
    spread = jnp.where(
        lax.broadcasted_iota(jnp.int32, (rows, members), 0) // group
        == lax.broadcasted_iota(jnp.int32, (rows, members), 1),
        1.0,
        0.0,
    ).astype(BF16)
    tall = lax.dot_general(
        spread, weight_ref[...], (((1,), (1,)), ((), ())), preferred_element_type=F32
    ).astype(BF16)
    wide = lax.dot_general(tall, spread, (((1,), (1,)), ((), ())), preferred_element_type=F32)
    same = (
        lax.broadcasted_iota(jnp.int32, (rows, rows), 0) % group
        == lax.broadcasted_iota(jnp.int32, (rows, rows), 1) % group
    )
    kron = jnp.where(same, wide, 0.0).astype(BF16)
    for start in range(0, cells, group):
        part = pl.ds(start, group)
        data = jnp.concatenate(
            [ref[i, part, :] for i in range(owners) for ref in (even_ref, odd_ref)], axis=0
        )
        sums = jnp.dot(kron, data, preferred_element_type=F32).astype(BF16)
        for i in range(members):
            out_ref[i, part, :] = sums[i * group : (i + 1) * group, :]


def place_body(in_ref, out_ref):
    lon = out_ref.shape[2]
    cells = in_ref.shape[2]
    for i in range(lon // cells):
        for m in range(out_ref.shape[0]):
            out_ref[m, 0, i * cells : (i + 1) * cells, :] = in_ref[i, m]


def body(latent, gains, conv, up, down, obs_cell, obs_chan, obs_value, obs_var):
    members, _, lon, ch = latent.shape
    count = obs_cell.shape[0]
    lat = lax.axis_size("lat")
    mem = lax.axis_size("mem")
    cell, chan = (v.reshape(1, count) for v in (obs_cell, obs_chan))
    value, var = (v.reshape(count // ch, ch) for v in (obs_value, obs_var))
    held = [pltpu.VMEM((lon, ch), BF16)]
    odd_row = (lax.axis_index("lat") % 2).reshape(1)
    work = 2 * lon * (9 * ch * ch + 2 * ch * up.shape[2])
    row = shaped((lon, ch), BF16)
    pair = shaped((members, lon, ch), BF16)
    cells = -(-lon // (mem * 16)) * 16

    def slot(m):
        return pl.BlockSpec((None, lon, ch), lambda i: (m, 0, 0))

    def halo(unit):
        pairs = [[(i, i + 1) for i in range(start, lat - 1, 2)] for start in (0, 1)]
        return [lax.ppermute(unit, "lat", p + [(j, i) for i, j in p]) for p in pairs]

    def block(b, m, x, before, mid, after, extra, outs, x_spec, halo_spec, scratch=()):
        return call(
            functools.partial(block_body, b, m),
            outs,
            (odd_row, x, before, mid, after, *held_weights, *extra),
            [SMEM, x_spec, halo_spec, halo_spec, halo_spec] + [VMEM] * (3 + len(extra)),
            grid=(1,),
            scratch=[*scratch, *held],
            mib=32,
            flops=work,
            nbytes=8 * lon * ch * 2,
        )

    def latent_spec(m):
        return pl.BlockSpec((None, None, lon, ch), lambda i: (m, 0, 0, 0))

    first, second = call(first_norm, (row, row), (latent, gains), nbytes=8 * lon * ch)
    before, after = halo(first)
    weights = (conv, up, down)
    held_weights = call(
        load_body,
        tuple(shaped(w.shape, BF16) for w in weights),
        weights,
        [HBM] * 3,
        scratch=[pltpu.SemaphoreType.DMA((24,))],
        mib=32,
        nbytes=sum(2 * w.size for w in weights),
    )
    fields_a, units = block(
        0, 0, latent, before, first, after, (gains, second), (row, pair), latent_spec(0), VMEM
    )
    before, after = halo(units)
    fields_b, last = block(
        0, 1, latent, before, units, after, (gains,), (row, row), latent_spec(1), slot(1)
    )
    plain = shaped((mem, cells, ch), BF16)
    with_seen = shaped((mem, cells + 8, ch), BF16)
    store = [pltpu.VMEM((mem * cells, ch), BF16)]
    fields_a, last = lax.optimization_barrier((fields_a, last))
    last_before, last_after = halo(last)
    even, seen = block(
        1,
        0,
        fields_a,
        before,
        units,
        after,
        (cell, chan),
        (plain, shaped((count // ch, ch), F32)),
        VMEM,
        slot(0),
        store,
    )
    even = lax.all_to_all(even, "mem", 0, 0, tiled=True)
    odd = block(
        1, 1, fields_b, last_before, last, last_after, (cell, chan, seen), with_seen, VMEM, VMEM, store
    )
    odd = lax.all_to_all(odd, "mem", 0, 0, tiled=True)

    def swap(v, axis, steps):
        size = {"lat": lat, "mem": mem}[axis]
        return [v] + [lax.ppermute(v, axis, [(i, i ^ s) for i in range(size)]) for s in steps]

    square = shaped((members * mem, 128), F32)
    terms = call(
        gram_body,
        square,
        (odd, value, var),
        [pl.BlockSpec((mem, 8, ch), lambda i: (0, cells // 8, 0)), VMEM, VMEM],
        grid=(1,),
    )
    terms = sum(swap(terms, "lat", (1, 2, 3)))
    sums = swap(terms, "lat", (4, 8, 12))
    weights = call(transform_body, shaped((members * mem, members * mem), BF16), sums)
    mixed = call(combine_body, shaped((members * mem, cells, ch), BF16), (weights, even, odd))
    mixed = lax.all_to_all(mixed.reshape(mem, members, cells, ch), "mem", 0, 0, tiled=True)
    return call(place_body, shaped(latent.shape, BF16), (mixed,))


def solution(mesh):
    in_specs = (
        P("mem", "lat", None, None),
        P(),
        P(),
        P(),
        P(),
        P("lat"),
        P("lat"),
        P("lat"),
        P("lat"),
    )
    out_specs = P("mem", "lat", None, None)
    return jax.shard_map(body, mesh=mesh, in_specs=in_specs, out_specs=out_specs, check_vma=False)
```

time: 244 us -> 141 us (0.58)
  the two profiles are of different devices: /device:TPU:0 before, /device:TPU:1 now
where the time goes in v1:
time: 141 us
  blocking collectives  59.9 us (42%)
  starting transfers between devices  30.6 us (22%)
  Pallas kernels  22.2 us (16%)
  waiting for transfers between devices  22.1 us (16%)
  local copies, waits for them, and re-layouts  5.95 us (4%)
    all_to_all x1, blocking collectives, body(): lax.all_to_all(mixed.reshape(mem, members, cells, ch), 'mem', 0, 0, tiled...  32.2 us
    all_to_all x1, blocking collectives, body(): odd = lax.all_to_all(odd, 'mem', 0, 0, tiled=True)  27.7 us
    pallas_call x10, Pallas kernels, call(): pl.pallas_call(body, out_shape=out_shape, in_specs=specs or [VMEM] * len(...  22.2 us
    ppermute x6, waiting for transfers between devices, halo(): lax.ppermute(unit, 'lat', p + [(j, i) for i, j in p])  15.4 us
    ppermute x6, starting transfers between devices, halo(): lax.ppermute(unit, 'lat', p + [(j, i) for i, j in p])  13.9 us
    ppermute x6, starting transfers between devices, swap(): lax.ppermute(v, axis, [(i, i ^ s) for i in range(size)])  13.3 us
    ppermute x6, waiting for transfers between devices, swap(): lax.ppermute(v, axis, [(i, i ^ s) for i in range(size)])  6.74 us
    unnamed x22, local copies, waits for them, and re-layouts  5.94 us
  transfers between devices with their start and end apart: 13, of which 6 were waited for; matrix products, arithmetic and copies ran while one was open for 0% of the time, Pallas kernels for 8%

profile of v1, /device:TPU:1, one launch (start us, length us, event | category | flops | bytes accessed | tf_op | source)
XLA Modules:
  0.0 141.0 jit_solution(14519323310934123788)
XLA Ops:
  0.0 0.0 copy-start
  0.0 1.1 copy-done
  1.1 0.0 copy-start.5
  1.1 0.7 copy-done.5
  1.8 0.0 copy-start.6
  1.8 0.3 shard_map.91
  2.1 0.0 copy-start.1
  2.1 2.2 %collective-permute-start = (bf16[720,256]{1,0:T(8,128)(2,1)S(1)}, bf16[720,256]{1,0:T(8,128)(2,1)S(1)}, u32[]{:S(2)}, u32[]{:S(2)}) collective-permute-start(bf16[720,256]{1,0:T(8,128)(2,1)S(1)} %get-tuple-element.18.mid_ref), channel_id=1, source_target_pairs={{0,16},{32,48},{64,80},{96,112},{128,144},{160,176},{192,208},{224... | collective-permute-start | bytes 1105928 | tf_op jit(solution)/shard_map/ppermute | solution.py:242
  4.4 0.7 collective-permute-start.1
  5.0 0.0 copy-start.2
  5.1 1.7 %copy-done.2 = bf16[2,2304,256]{2,1,0:T(8,128)(2,1)S(1)} copy-done((bf16[2,2304,256]{2,1,0:T(8,128)(2,1)S(1)}, bf16[2,2304,256]{2,1,0:T(8,128)(2,1)}, u32[]{:S(2)}) %copy-start.2) | copy-done | bytes 2359320
  6.7 0.0 copy-start.3
  6.7 1.2 copy-done.3
  7.9 0.0 copy-start.4
  7.9 1.2 copy-done.4
  9.2 3.4 %shard_map.92 = (bf16[2,2304,256]{2,1,0:T(8,128)(2,1)S(1)}, bf16[2,256,1024]{2,1,0:T(8,128)(2,1)S(1)}, bf16[2,1024,256]{2,1,0:T(8,128)(2,1)S(1)}) custom-call(bf16[2,2304,256]{2,1,0:T(8,128)(2,1)S(1)} %copy-done.2, bf16[2,256,1024]{2,1,0:T(8,128)(2,1)S(1)} %copy-done.3, bf16[2,1024,256]{2,1,0:T(8,128)(2,1)S(1)} %copy-done.4), custom_call_target="tpu_custom_call" | custom-call | bytes 4456448 | tf_op jit(solution)/shard_map/pallas_call | solution.py:22
  12.6 0.0 collective-permute-done.near_ref
  12.6 0.0 collective-permute-done.1.far_ref
  12.6 0.0 copy-done.6
  12.6 0.0 copy-done.1
  12.6 3.0 %shard_map.93 = (bf16[720,256]{1,0:T(8,128)(2,1)S(1)}, bf16[2,720,256]{2,1,0:T(8,128)(2,1)S(1)}) custom-call(s32[1]{0:T(128)} %bitcast.odd_ref, bf16[2,1,720,256]{3,2,1,0:T(8,128)(2,1)S(1)} %copy-done.1, bf16[720,256]{1,0:T(8,128)(2,1)S(1)} %collective-permute-done.near_ref, bf16[720,256]{1,0:T(8,128)(2,1)S(1)} %get-tuple-element.18.mid_ref, ...), custom_call_target="tpu_custom_call" | custom-call | flops 1604321280 | bytes 2949120 | tf_op jit(solution)/shard_map/pallas_call | solution.py:22
  15.7 0.0 copy-start.7
  15.7 0.0 copy-start.8
  15.7 3.6 %collective-permute-start.2 = (bf16[2,720,256]{2,1,0:T(8,128)(2,1)S(1)}, bf16[2,720,256]{2,1,0:T(8,128)(2,1)S(1)}, u32[]{:S(2)}, u32[]{:S(2)}) collective-permute-start(bf16[2,720,256]{2,1,0:T(8,128)(2,1)S(1)} %get-tuple-element.23.mid_ref), channel_id=1, source_target_pairs={{0,16},{32,48},{64,80},{96,112},{128,144},{160,176},{192,208},{224... | collective-permute-start | bytes 2211848 | tf_op jit(solution)/shard_map/ppermute | solution.py:242
  19.3 0.7 collective-permute-start.3
  20.0 14.2 %collective-permute-done.2.near_ref = bf16[2,720,256]{2,1,0:T(8,128)(2,1)S(1)} collective-permute-done((bf16[2,720,256]{2,1,0:T(8,128)(2,1)S(1)}, bf16[2,720,256]{2,1,0:T(8,128)(2,1)S(1)}, u32[]{:S(2)}, u32[]{:S(2)}) %collective-permute-start.2) | collective-permute-done | bytes 737312 | tf_op jit(solution)/shard_map/ppermute | solution.py:242
  34.2 0.0 collective-permute-done.3.far_ref
  34.2 3.0 %shard_map.94 = (bf16[720,256]{1,0:T(8,128)(2,1)S(1)}, bf16[720,256]{1,0:T(8,128)(2,1)S(1)}) custom-call(s32[1]{0:T(128)} %bitcast.odd_ref, bf16[2,1,720,256]{3,2,1,0:T(8,128)(2,1)S(1)} %copy-done.1, bf16[2,720,256]{2,1,0:T(8,128)(2,1)S(1)} %collective-permute-done.2.near_ref, bf16[2,720,256]{2,1,0:T(8,128)(2,1)S(1)} %get-tuple-element.23.mid_ref, ...), custom_call_target="tpu_custom_call" | custom-call | flops 1604321280 | bytes 2949120 | tf_op jit(solution)/shard_map/pallas_call | solution.py:22
  37.2 5.8 %collective-permute-start.4 = (bf16[720,256]{1,0:T(8,128)(2,1)S(1)}, bf16[720,256]{1,0:T(8,128)(2,1)S(1)}, u32[]{:S(2)}, u32[]{:S(2)}) collective-permute-start(bf16[720,256]{1,0:T(8,128)(2,1)S(1)} %get-tuple-element.27.mid_ref), channel_id=1, source_target_pairs={{0,16},{32,48},{64,80},{96,112},{128,144},{160,176},{192,208},{224... | collective-permute-start | bytes 1105928 | tf_op jit(solution)/shard_map/ppermute | solution.py:242
  43.0 0.9 collective-permute-start.5
  43.9 0.0 copy-done.7
  43.9 0.0 copy-done.8
  43.9 4.0 %shard_map.95 = (bf16[16,48,256]{2,1,0:T(8,128)(2,1)}, f32[4,256]{1,0:T(4,128)S(1)}) custom-call(s32[1]{0:T(128)} %bitcast.odd_ref, bf16[720,256]{1,0:T(8,128)(2,1)S(1)} %get-tuple-element.28.x_ref, bf16[2,720,256]{2,1,0:T(8,128)(2,1)S(1)} %collective-permute-done.2.near_ref, bf16[2,720,256]{2,1,0:T(8,128)(2,1)S(1)} %get-tuple-element.23.mid_ref, ...), custom_call_target="tpu_custom_call" | custom-call | flops 1604321280 | bytes 2949120 | tf_op jit(solution)/shard_map/pallas_call | solution.py:22
  48.0 1.2 collective-permute-done.4.near_ref
  49.2 0.0 collective-permute-done.5.far_ref
  49.2 0.0 copy-start.9
  49.2 0.0 copy-start.10
  49.2 3.4 %shard_map.96 = bf16[16,56,256]{2,1,0:T(8,128)(2,1)S(1)} custom-call(s32[1]{0:T(128)} %bitcast.odd_ref, bf16[720,256]{1,0:T(8,128)(2,1)S(1)} %get-tuple-element.24.x_ref, bf16[720,256]{1,0:T(8,128)(2,1)S(1)} %collective-permute-done.4.near_ref, bf16[720,256]{1,0:T(8,128)(2,1)S(1)} %get-tuple-element.27.mid_ref, ...), custom_call_target="tpu_custom_call" | custom-call | flops 1604321280 | bytes 2949120 | tf_op jit(solution)/shard_map/pallas_call | solution.py:22
  52.5 27.7 %all_to_all.15.seen_ref.odd_ref = bf16[16,56,256]{2,1,0:T(8,128)(2,1)S(1)} all-to-all(bf16[16,56,256]{2,1,0:T(8,128)(2,1)S(1)} %shard_map.96), channel_id=1, replica_groups=mesh['lat'=16,'mem'=16] {'mem'}, dimensions={0} | all-to-all | bytes 917504 | tf_op jit(solution)/shard_map/all_to_all | solution.py:301
  80.2 3.5 %all-to-all-start.1 = ((bf16[16,48,256]{2,1,0:T(8,128)(2,1)}), bf16[16,48,256]{2,1,0:T(8,128)(2,1)S(1)}, u32[]{:S(2)}, u32[]{:S(2)}) async-start(bf16[16,48,256]{2,1,0:T(8,128)(2,1)} %get-tuple-element.30), calls=%async_computation.1 | async-start | bytes 786432 | tf_op jit(solution)/shard_map/all_to_all | solution.py:297
  83.7 0.0 copy-done.9
  83.7 0.0 copy-done.10
  83.7 0.8 shard_map.97
  84.5 5.5 %collective-permute-start.6 = (f32[32,128]{1,0:T(8,128)S(1)}, f32[32,128]{1,0:T(8,128)S(1)}, u32[]{:S(2)}, u32[]{:S(2)}) collective-permute-start(f32[32,128]{1,0:T(8,128)S(1)} %shard_map.97), channel_id=1, source_target_pairs={{0,16},{16,0},{32,48},{48,32},{64,80},{80,64},{96,112},{112,96},{1... | collective-permute-start | bytes 49160 | tf_op jit(solution)/shard_map/ppermute | solution.py:305
  90.0 3.9 %collective-permute-start.7 = (f32[32,128]{1,0:T(8,128)S(1)}, f32[32,128]{1,0:T(8,128)S(1)}, u32[]{:S(2)}, u32[]{:S(2)}) collective-permute-start(f32[32,128]{1,0:T(8,128)S(1)} %shard_map.97), channel_id=1, source_target_pairs={{0,32},{16,48},{32,0},{48,16},{64,96},{80,112},{96,64},{112,80},{1... | collective-permute-start | bytes 49160 | tf_op jit(solution)/shard_map/ppermute | solution.py:305
  93.9 0.0 collective-permute-start.8
  93.9 0.0 collective-permute-done.6
  93.9 1.9 %collective-permute-done.7 = f32[32,128]{1,0:T(8,128)S(1)} collective-permute-done((f32[32,128]{1,0:T(8,128)S(1)}, f32[32,128]{1,0:T(8,128)S(1)}, u32[]{:S(2)}, u32[]{:S(2)}) %collective-permute-start.7) | collective-permute-done | bytes 16416 | tf_op jit(solution)/shard_map/ppermute | solution.py:305
  95.8 1.9 %collective-permute-done.8 = f32[32,128]{1,0:T(8,128)S(1)} collective-permute-done((f32[32,128]{1,0:T(8,128)S(1)}, f32[32,128]{1,0:T(8,128)S(1)}, u32[]{:S(2)}, u32[]{:S(2)}) %collective-permute-start.8) | collective-permute-done | bytes 16416 | tf_op jit(solution)/shard_map/ppermute | solution.py:305
  97.7 3.1 %collective-permute-start.10 = (f32[32,128]{1,0:T(8,128)S(1)}, f32[32,128]{1,0:T(8,128)S(1)}, u32[]{:S(2)}, u32[]{:S(2)}) collective-permute-start(f32[32,128]{1,0:T(8,128)S(1)} %add_add_fusion.a_ref), channel_id=1, source_target_pairs={{0,128},{16,144},{32,160},{48,176},{64,192},{80,208},{96,224},{112... | collective-permute-start | bytes 49160 | tf_op jit(solution)/shard_map/ppermute | solution.py:305
  100.8 0.9 collective-permute-start.11
  101.6 0.0 collective-permute-start.9
  101.6 0.3 collective-permute-done.10.c_ref
  101.9 2.7 %collective-permute-done.11.d_ref = f32[32,128]{1,0:T(8,128)S(1)} collective-permute-done((f32[32,128]{1,0:T(8,128)S(1)}, f32[32,128]{1,0:T(8,128)S(1)}, u32[]{:S(2)}, u32[]{:S(2)}) %collective-permute-start.11) | collective-permute-done | bytes 16416 | tf_op jit(solution)/shard_map/ppermute | solution.py:305
  104.6 0.0 collective-permute-done.9.b_ref
  104.6 2.5 %shard_map.98.weight_ref = bf16[32,32]{1,0:T(8,128)(2,1)S(1)} custom-call(f32[32,128]{1,0:T(8,128)S(1)} %add_add_fusion.a_ref, f32[32,128]{1,0:T(8,128)S(1)} %collective-permute-done.9.b_ref, f32[32,128]{1,0:T(8,128)S(1)} %collective-permute-done.10.c_ref, f32[32,128]{1,0:T(8,128)S(1)} %collective-permute-done.11.d_ref), custom_call_target="tpu_custom_call" | custom-call | tf_op jit(solution)/shard_map/pallas_call | solution.py:22
  107.0 0.0 all-to-all-done.1.even_ref
  107.0 0.8 shard_map.99
  107.9 32.2 %all_to_all.16.in_ref = bf16[16,2,48,256]{3,2,1,0:T(8,128)(2,1)S(1)} all-to-all(bf16[16,2,48,256]{3,2,1,0:T(8,128)(2,1)S(1)} %bitcast.4), channel_id=1, replica_groups=mesh['lat'=16,'mem'=16] {'mem'}, dimensions={0} | all-to-all | bytes 1572864 | tf_op jit(solution)/shard_map/all_to_all | solution.py:319
  140.0 0.9 shard_map.100
  (3 shorter events, 0.0 us)
Async XLA Ops:
  0.0 1.1 copy-start
  1.1 0.7 copy-start.5
  1.8 10.8 %copy-start.6 = (f32[2,256]{1,0:T(2,128)S(1)}, f32[2,256]{1,0:T(2,128)}, u32[]{:S(2)}) copy-start(f32[2,256]{1,0:T(2,128)} %rest_0_.3) | copy-start | bytes 6148
  2.1 10.5 %copy-start.1 = (bf16[2,1,720,256]{3,2,1,0:T(8,128)(2,1)S(1)}, bf16[2,1,720,256]{3,2,1,0:T(8,128)(2,1)}, u32[]{:S(2)}) copy-start(bf16[2,1,720,256]{3,2,1,0:T(8,128)(2,1)} %x_ref.5) | copy-start | bytes 2211844
  2.1 10.5 %collective-permute-start = (bf16[720,256]{1,0:T(8,128)(2,1)S(1)}, bf16[720,256]{1,0:T(8,128)(2,1)S(1)}, u32[]{:S(2)}, u32[]{:S(2)}) collective-permute-start(bf16[720,256]{1,0:T(8,128)(2,1)S(1)} %get-tuple-element.18.mid_ref), channel_id=1, source_target_pairs={{0,16},{32,48},{64,80},{96,112},{128,144},{160,176},{192,208},{224... | collective-permute-start | bytes 1105928 | tf_op jit(solution)/shard_map/ppermute | solution.py:242
  4.4 8.3 %collective-permute-start.1 = (bf16[720,256]{1,0:T(8,128)(2,1)S(1)}, bf16[720,256]{1,0:T(8,128)(2,1)S(1)}, u32[]{:S(2)}, u32[]{:S(2)}) collective-permute-start(bf16[720,256]{1,0:T(8,128)(2,1)S(1)} %get-tuple-element.18.mid_ref), channel_id=1, source_target_pairs={{16,32},{48,64},{80,96},{112,128},{144,160},{176,192},{208,224},{3... | collective-permute-start | bytes 1105928 | tf_op jit(solution)/shard_map/ppermute | solution.py:242
  5.0 1.7 %copy-start.2 = (bf16[2,2304,256]{2,1,0:T(8,128)(2,1)S(1)}, bf16[2,2304,256]{2,1,0:T(8,128)(2,1)}, u32[]{:S(2)}) copy-start(bf16[2,2304,256]{2,1,0:T(8,128)(2,1)} %refs_0_.1) | copy-start | bytes 7077892
  6.7 1.2 copy-start.3
  7.9 1.2 copy-start.4
  15.7 28.2 %copy-start.7 = (s32[1024]{0:T(1024)S(1)}, s32[1024]{0:T(1024)}, u32[]{:S(2)}) copy-start(s32[1024]{0:T(1024)} %param.14) | copy-start | bytes 12292
  15.7 28.2 %copy-start.8 = (s32[1024]{0:T(1024)S(1)}, s32[1024]{0:T(1024)}, u32[]{:S(2)}) copy-start(s32[1024]{0:T(1024)} %param.15) | copy-start | bytes 12292
  15.7 18.5 %collective-permute-start.2 = (bf16[2,720,256]{2,1,0:T(8,128)(2,1)S(1)}, bf16[2,720,256]{2,1,0:T(8,128)(2,1)S(1)}, u32[]{:S(2)}, u32[]{:S(2)}) collective-permute-start(bf16[2,720,256]{2,1,0:T(8,128)(2,1)S(1)} %get-tuple-element.23.mid_ref), channel_id=1, source_target_pairs={{0,16},{32,48},{64,80},{96,112},{128,144},{160,176},{192,208},{224... | collective-permute-start | bytes 2211848 | tf_op jit(solution)/shard_map/ppermute | solution.py:242
  19.3 14.9 %collective-permute-start.3 = (bf16[2,720,256]{2,1,0:T(8,128)(2,1)S(1)}, bf16[2,720,256]{2,1,0:T(8,128)(2,1)S(1)}, u32[]{:S(2)}, u32[]{:S(2)}) collective-permute-start(bf16[2,720,256]{2,1,0:T(8,128)(2,1)S(1)} %get-tuple-element.23.mid_ref), channel_id=1, source_target_pairs={{16,32},{48,64},{80,96},{112,128},{144,160},{176,192},{208,224},{3... | collective-permute-start | bytes 2211848 | tf_op jit(solution)/shard_map/ppermute | solution.py:242
  37.2 11.9 %collective-permute-start.4 = (bf16[720,256]{1,0:T(8,128)(2,1)S(1)}, bf16[720,256]{1,0:T(8,128)(2,1)S(1)}, u32[]{:S(2)}, u32[]{:S(2)}) collective-permute-start(bf16[720,256]{1,0:T(8,128)(2,1)S(1)} %get-tuple-element.27.mid_ref), channel_id=1, source_target_pairs={{0,16},{32,48},{64,80},{96,112},{128,144},{160,176},{192,208},{224... | collective-permute-start | bytes 1105928 | tf_op jit(solution)/shard_map/ppermute | solution.py:242
  43.0 6.1 %collective-permute-start.5 = (bf16[720,256]{1,0:T(8,128)(2,1)S(1)}, bf16[720,256]{1,0:T(8,128)(2,1)S(1)}, u32[]{:S(2)}, u32[]{:S(2)}) collective-permute-start(bf16[720,256]{1,0:T(8,128)(2,1)S(1)} %get-tuple-element.27.mid_ref), channel_id=1, source_target_pairs={{16,32},{48,64},{80,96},{112,128},{144,160},{176,192},{208,224},{3... | collective-permute-start | bytes 1105928 | tf_op jit(solution)/shard_map/ppermute | solution.py:242
  49.2 34.5 %copy-start.9 = (f32[1024]{0:T(1024)S(1)}, f32[1024]{0:T(1024)}, u32[]{:S(2)}) copy-start(f32[1024]{0:T(1024)} %param.16) | copy-start | bytes 12292
  49.2 34.5 %copy-start.10 = (f32[1024]{0:T(1024)S(1)}, f32[1024]{0:T(1024)}, u32[]{:S(2)}) copy-start(f32[1024]{0:T(1024)} %param.17) | copy-start | bytes 12292
  80.2 26.8 %all-to-all-start.1 = ((bf16[16,48,256]{2,1,0:T(8,128)(2,1)}), bf16[16,48,256]{2,1,0:T(8,128)(2,1)S(1)}, u32[]{:S(2)}, u32[]{:S(2)}) async-start(bf16[16,48,256]{2,1,0:T(8,128)(2,1)} %get-tuple-element.30), calls=%async_computation.1 | async-start | bytes 786432 | tf_op jit(solution)/shard_map/all_to_all | solution.py:297
  84.5 9.4 %collective-permute-start.6 = (f32[32,128]{1,0:T(8,128)S(1)}, f32[32,128]{1,0:T(8,128)S(1)}, u32[]{:S(2)}, u32[]{:S(2)}) collective-permute-start(f32[32,128]{1,0:T(8,128)S(1)} %shard_map.97), channel_id=1, source_target_pairs={{0,16},{16,0},{32,48},{48,32},{64,80},{80,64},{96,112},{112,96},{1... | collective-permute-start | bytes 49160 | tf_op jit(solution)/shard_map/ppermute | solution.py:305
  90.0 5.8 %collective-permute-start.7 = (f32[32,128]{1,0:T(8,128)S(1)}, f32[32,128]{1,0:T(8,128)S(1)}, u32[]{:S(2)}, u32[]{:S(2)}) collective-permute-start(f32[32,128]{1,0:T(8,128)S(1)} %shard_map.97), channel_id=1, source_target_pairs={{0,32},{16,48},{32,0},{48,16},{64,96},{80,112},{96,64},{112,80},{1... | collective-permute-start | bytes 49160 | tf_op jit(solution)/shard_map/ppermute | solution.py:305
  93.9 3.8 %collective-permute-start.8 = (f32[32,128]{1,0:T(8,128)S(1)}, f32[32,128]{1,0:T(8,128)S(1)}, u32[]{:S(2)}, u32[]{:S(2)}) collective-permute-start(f32[32,128]{1,0:T(8,128)S(1)} %shard_map.97), channel_id=1, source_target_pairs={{0,48},{16,32},{32,16},{48,0},{64,112},{80,96},{96,80},{112,64},{1... | collective-permute-start | bytes 49160 | tf_op jit(solution)/shard_map/ppermute | solution.py:305
  97.7 4.2 %collective-permute-start.10 = (f32[32,128]{1,0:T(8,128)S(1)}, f32[32,128]{1,0:T(8,128)S(1)}, u32[]{:S(2)}, u32[]{:S(2)}) collective-permute-start(f32[32,128]{1,0:T(8,128)S(1)} %add_add_fusion.a_ref), channel_id=1, source_target_pairs={{0,128},{16,144},{32,160},{48,176},{64,192},{80,208},{96,224},{112... | collective-permute-start | bytes 49160 | tf_op jit(solution)/shard_map/ppermute | solution.py:305
  100.8 3.8 %collective-permute-start.11 = (f32[32,128]{1,0:T(8,128)S(1)}, f32[32,128]{1,0:T(8,128)S(1)}, u32[]{:S(2)}, u32[]{:S(2)}) collective-permute-start(f32[32,128]{1,0:T(8,128)S(1)} %add_add_fusion.a_ref), channel_id=1, source_target_pairs={{0,192},{16,208},{32,224},{48,240},{64,128},{80,144},{96,160},{112... | collective-permute-start | bytes 49160 | tf_op jit(solution)/shard_map/ppermute | solution.py:305
  101.6 2.9 %collective-permute-start.9 = (f32[32,128]{1,0:T(8,128)S(1)}, f32[32,128]{1,0:T(8,128)S(1)}, u32[]{:S(2)}, u32[]{:S(2)}) collective-permute-start(f32[32,128]{1,0:T(8,128)S(1)} %add_add_fusion.a_ref), channel_id=1, source_target_pairs={{0,64},{16,80},{32,96},{48,112},{64,0},{80,16},{96,32},{112,48},{1... | collective-permute-start | bytes 49160 | tf_op jit(solution)/shard_map/ppermute | solution.py:305

commit v2 on v1

--- a/solution.py
+++ b/solution.py
@@ -69,11 +69,7 @@
     if last and member == 0:
         cell_ref, chan_ref, out_ref, seen_ref, fields_ref = rest
     elif last:
-        cell_ref, chan_ref, seen_ref, out_ref, fields_ref = rest
-    elif member == 0:
-        gain_ref, later_ref, fields_ref, pair_ref = rest
-        unit_ref = pair_ref.at[0]
-        pair_ref[1] = later_ref[...]
+        cell_ref, chan_ref, first_ref, seen_ref, out_ref, all_seen_ref, fields_ref = rest
     else:
         gain_ref, fields_ref, unit_ref = rest
     lon, ch = x_ref.shape
@@ -111,13 +107,16 @@
         seen = [seen[:, i : i + ch] for i in range(0, count, ch)]
         fields_ref[lon:, :] = jnp.zeros((owners * cells - lon, ch), BF16)
         for i in range(owners):
-            out_ref[i, :cells, :] = fields_ref[i * cells : (i + 1) * cells, :]
+            out_ref[i, member * cells : (member + 1) * cells, :] = fields_ref[
+                i * cells : (i + 1) * cells, :
+            ]
         if member == 0:
             seen_ref[...] = jnp.concatenate(seen, axis=0)
         else:
             both = jnp.concatenate([seen_ref[...], *seen], axis=0).astype(BF16)
             for i in range(owners):
-                out_ref[i, cells:, :] = both
+                out_ref[i, :cells, :] = first_ref[i]
+                all_seen_ref[i] = both
 
 
 def gram_body(seen_ref, value_ref, var_ref, out_ref):
@@ -181,9 +180,9 @@
     out_ref[...] = (weights + (1.0 - totals) / members).astype(BF16)
 
 
-def combine_body(weight_ref, even_ref, odd_ref, out_ref):
+def combine_body(weight_ref, share_ref, out_ref):
     members = weight_ref.shape[0]
-    owners = even_ref.shape[0]
+    owners = share_ref.shape[0]
     cells = out_ref.shape[1]
     group = 16
     rows = members * group
@@ -205,7 +204,8 @@
     for start in range(0, cells, group):
         part = pl.ds(start, group)
         data = jnp.concatenate(
-            [ref[i, part, :] for i in range(owners) for ref in (even_ref, odd_ref)], axis=0
+            [share_ref[i, pl.ds(m * cells + start, group), :] for i in range(owners) for m in range(2)],
+            axis=0,
         )
         sums = jnp.dot(kron, data, preferred_element_type=F32).astype(BF16)
         for i in range(members):
@@ -231,21 +231,17 @@
     odd_row = (lax.axis_index("lat") % 2).reshape(1)
     work = 2 * lon * (9 * ch * ch + 2 * ch * up.shape[2])
     row = shaped((lon, ch), BF16)
-    pair = shaped((members, lon, ch), BF16)
     cells = -(-lon // (mem * 16)) * 16
-
-    def slot(m):
-        return pl.BlockSpec((None, lon, ch), lambda i: (m, 0, 0))
 
     def halo(unit):
         pairs = [[(i, i + 1) for i in range(start, lat - 1, 2)] for start in (0, 1)]
         return [lax.ppermute(unit, "lat", p + [(j, i) for i, j in p]) for p in pairs]
 
-    def block(b, m, x, before, mid, after, extra, outs, x_spec, halo_spec, scratch=()):
+    def block(b, m, x, near, mid, far, extra, outs, x_spec, halo_spec, scratch=()):
         return call(
             functools.partial(block_body, b, m),
             outs,
-            (odd_row, x, before, mid, after, *held_weights, *extra),
+            (odd_row, x, near, mid, far, *held_weights, *extra),
             [SMEM, x_spec, halo_spec, halo_spec, halo_spec] + [VMEM] * (3 + len(extra)),
             grid=(1,),
             scratch=[*scratch, *held],
@@ -257,8 +253,8 @@
     def latent_spec(m):
         return pl.BlockSpec((None, None, lon, ch), lambda i: (m, 0, 0, 0))
 
-    first, second = call(first_norm, (row, row), (latent, gains), nbytes=8 * lon * ch)
-    before, after = halo(first)
+    units = call(first_norm, (row,) * members, (latent, gains), nbytes=8 * lon * ch)
+    firsts = [(unit, *halo(unit)) for unit in units]
     weights = (conv, up, down)
     held_weights = call(
         load_body,
@@ -266,39 +262,31 @@
         weights,
         [HBM] * 3,
         scratch=[pltpu.SemaphoreType.DMA((24,))],
-        mib=32,
+        mib=50,
         nbytes=sum(2 * w.size for w in weights),
     )
-    fields_a, units = block(
-        0, 0, latent, before, first, after, (gains, second), (row, pair), latent_spec(0), VMEM
-    )
-    before, after = halo(units)
-    fields_b, last = block(
-        0, 1, latent, before, units, after, (gains,), (row, row), latent_spec(1), slot(1)
-    )
+    fields, lasts = [], []
+    for m, (unit, near, far) in enumerate(firsts):
+        out, unit = block(
+            0, m, latent, near, unit, far, (gains,), (row, row), latent_spec(m), VMEM
+        )
+        fields.append(out)
+        lasts.append((unit, *halo(unit)))
     plain = shaped((mem, cells, ch), BF16)
-    with_seen = shaped((mem, cells + 8, ch), BF16)
+    both = shaped((mem, members * cells, ch), BF16)
     store = [pltpu.VMEM((mem * cells, ch), BF16)]
-    fields_a, last = lax.optimization_barrier((fields_a, last))
-    last_before, last_after = halo(last)
-    even, seen = block(
-        1,
-        0,
-        fields_a,
-        before,
-        units,
-        after,
-        (cell, chan),
-        (plain, shaped((count // ch, ch), F32)),
-        VMEM,
-        slot(0),
-        store,
-    )
-    even = lax.all_to_all(even, "mem", 0, 0, tiled=True)
-    odd = block(
-        1, 1, fields_b, last_before, last, last_after, (cell, chan, seen), with_seen, VMEM, VMEM, store
-    )
-    odd = lax.all_to_all(odd, "mem", 0, 0, tiled=True)
+    fields[0], _ = lax.optimization_barrier((fields[0], lasts[1][0]))
+    unit, near, far = lasts[0]
+    outs = (plain, shaped((count // ch, ch), F32))
+    even, seen = block(1, 0, fields[0], near, unit, far, (cell, chan), outs, VMEM, VMEM, store)
+    unit, near, far = lasts[1]
+    outs = (both, shaped((mem, 8, ch), BF16))
+    share, seen = block(
+        1, 1, fields[1], near, unit, far, (cell, chan, even, seen), outs, VMEM, VMEM, store
+    )
+    seen = lax.all_to_all(seen, "mem", 0, 0, tiled=True)
+    share, seen = lax.optimization_barrier((share, seen))
+    share = lax.all_to_all(share, "mem", 0, 0, tiled=True)
 
     def swap(v, axis, steps):
         size = {"lat": lat, "mem": mem}[axis]
@@ -308,14 +296,12 @@
     terms = call(
         gram_body,
         square,
-        (odd, value, var),
-        [pl.BlockSpec((mem, 8, ch), lambda i: (0, cells // 8, 0)), VMEM, VMEM],
-        grid=(1,),
+        (seen, value, var),
     )
     terms = sum(swap(terms, "lat", (1, 2, 3)))
     sums = swap(terms, "lat", (4, 8, 12))
     weights = call(transform_body, shaped((members * mem, members * mem), BF16), sums)
-    mixed = call(combine_body, shaped((members * mem, cells, ch), BF16), (weights, even, odd))
+    mixed = call(combine_body, shaped((members * mem, cells, ch), BF16), (weights, share))
     mixed = lax.all_to_all(mixed.reshape(mem, members, cells, ch), "mem", 0, 0, tiled=True)
     return call(place_body, shaped(latent.shape, BF16), (mixed,))
 

time: 141 us -> 119 us (0.84)
  blocking collectives: 59.9 us -> 46.4 us
  waiting for transfers between devices: 22.1 us -> 15.7 us
  starting transfers between devices: 30.6 us -> 28.7 us
    ppermute x6 -> x8, waiting for transfers between devices: 15.4 us -> 3.35 us  [halo(): lax.ppermute(unit, 'lat', p + [(j, i) for i, j in p])]
    all_to_all x1, blocking collectives: 27.7 us -> 19.8 us  [body(): seen = lax.all_to_all(seen, 'mem', 0, 0, tiled=True)]
    ppermute x6, starting transfers between devices: 13.3 us -> 7.01 us  [swap(): lax.ppermute(v, axis, [(i, i ^ s) for i in range(size)])]
    all_to_all x1, waiting for transfers between devices: 0.01 us -> 6.03 us  [body(): share = lax.all_to_all(share, 'mem', 0, 0, tiled=True)]
    all_to_all x1, blocking collectives: 32.2 us -> 26.5 us  [body(): lax.all_to_all(mixed.reshape(mem, members, cells, ch), 'mem', 0, 0, tiled...]
    ppermute x6 -> x8, starting transfers between devices: 13.9 us -> 18.2 us  [halo(): lax.ppermute(unit, 'lat', p + [(j, i) for i, j in p])]
  transfers between devices with their start and end apart: 13 -> 15, of which waited for: 6 -> 7; matrix products, arithmetic and copies ran while one was open for 0% -> 0% of each run, Pallas kernels for 8% -> 14%
where the time goes in v2:
time: 119 us
  blocking collectives  46.4 us (39%)
  starting transfers between devices  28.7 us (24%)
  Pallas kernels  23.1 us (19%)
  waiting for transfers between devices  15.7 us (13%)
  local copies, waits for them, and re-layouts  4.73 us (4%)
    all_to_all x1, blocking collectives, body(): lax.all_to_all(mixed.reshape(mem, members, cells, ch), 'mem', 0, 0, tiled...  26.5 us
    pallas_call x10, Pallas kernels, call(): pl.pallas_call(body, out_shape=out_shape, in_specs=specs or [VMEM] * len(...  23.1 us
    all_to_all x1, blocking collectives, body(): seen = lax.all_to_all(seen, 'mem', 0, 0, tiled=True)  19.8 us
    ppermute x8, starting transfers between devices, halo(): lax.ppermute(unit, 'lat', p + [(j, i) for i, j in p])  18.2 us
    ppermute x6, starting transfers between devices, swap(): lax.ppermute(v, axis, [(i, i ^ s) for i in range(size)])  7.01 us
    ppermute x6, waiting for transfers between devices, swap(): lax.ppermute(v, axis, [(i, i ^ s) for i in range(size)])  6.36 us
    all_to_all x1, waiting for transfers between devices, body(): share = lax.all_to_all(share, 'mem', 0, 0, tiled=True)  6.03 us
    unnamed x22, local copies, waits for them, and re-layouts  4.71 us
  transfers between devices with their start and end apart: 15, of which 7 were waited for; matrix products, arithmetic and copies ran while one was open for 0% of the time, Pallas kernels for 14%

profile of v2, /device:TPU:1, one launch (start us, length us, event | category | flops | bytes accessed | tf_op | source)
XLA Modules:
  0.0 118.9 jit_solution(7436474006580564301)
XLA Ops:
  0.0 0.0 copy-start.2
  0.0 1.1 copy-done.2
  1.1 0.0 copy-start.5
  1.1 0.7 copy-done.5
  1.8 0.0 copy-start.6
  1.8 0.3 shard_map.91
  2.1 0.0 copy-start.3
  2.1 0.8 collective-permute-start.5
  3.0 4.7 %collective-permute-start.4 = (bf16[720,256]{1,0:T(8,128)(2,1)S(1)}, bf16[720,256]{1,0:T(8,128)(2,1)S(1)}, u32[]{:S(2)}, u32[]{:S(2)}) collective-permute-start(bf16[720,256]{1,0:T(8,128)(2,1)S(1)} %get-tuple-element.27.mid_ref), channel_id=1, source_target_pairs={{0,16},{32,48},{64,80},{96,112},{128,144},{160,176},{192,208},{224... | collective-permute-start | bytes 1105928 | tf_op jit(solution)/shard_map/ppermute | solution.py:238
  7.7 0.7 collective-permute-start.1
  8.4 3.2 %collective-permute-start = (bf16[720,256]{1,0:T(8,128)(2,1)S(1)}, bf16[720,256]{1,0:T(8,128)(2,1)S(1)}, u32[]{:S(2)}, u32[]{:S(2)}) collective-permute-start(bf16[720,256]{1,0:T(8,128)(2,1)S(1)} %get-tuple-element.21.mid_ref), channel_id=1, source_target_pairs={{0,16},{32,48},{64,80},{96,112},{128,144},{160,176},{192,208},{224... | collective-permute-start | bytes 1105928 | tf_op jit(solution)/shard_map/ppermute | solution.py:238
  11.6 0.0 copy-start.4
  11.6 1.2 %copy-done.4 = bf16[2,256,1024]{2,1,0:T(8,128)(2,1)S(1)} copy-done((bf16[2,256,1024]{2,1,0:T(8,128)(2,1)S(1)}, bf16[2,256,1024]{2,1,0:T(8,128)(2,1)}, u32[]{:S(2)}) %copy-start.4) | copy-done | bytes 1048600
  12.8 4.2 %shard_map.92 = (bf16[2,2304,256]{2,1,0:T(8,128)(2,1)}, bf16[2,256,1024]{2,1,0:T(8,128)(2,1)S(1)}, bf16[2,1024,256]{2,1,0:T(8,128)(2,1)S(1)}) custom-call(bf16[2,2304,256]{2,1,0:T(8,128)(2,1)} %refs_0_.1, bf16[2,256,1024]{2,1,0:T(8,128)(2,1)S(1)} %copy-done.4, bf16[2,1024,256]{2,1,0:T(8,128)(2,1)} %refs_2_.1), custom_call_target="tpu_custom_call" | custom-call | bytes 4456448 | tf_op jit(solution)/shard_map/pallas_call | solution.py:22
  17.0 0.0 collective-permute-done.5.far_ref
  17.0 0.0 collective-permute-done.4.near_ref
  17.0 0.0 copy-done.6
  17.0 0.0 copy-done.3
  17.0 0.0 copy-start
  17.0 1.7 %copy-done = bf16[2,2304,256]{2,1,0:T(8,128)(2,1)S(1)} copy-done((bf16[2,2304,256]{2,1,0:T(8,128)(2,1)S(1)}, bf16[2,2304,256]{2,1,0:T(8,128)(2,1)}, u32[]{:S(2)}) %copy-start) | copy-done | bytes 2359320
  18.7 3.0 %shard_map.94 = (bf16[720,256]{1,0:T(8,128)(2,1)S(1)}, bf16[720,256]{1,0:T(8,128)(2,1)S(1)}) custom-call(s32[1]{0:T(128)} %bitcast.odd_ref, bf16[2,1,720,256]{3,2,1,0:T(8,128)(2,1)S(1)} %copy-done.3, bf16[720,256]{1,0:T(8,128)(2,1)S(1)} %collective-permute-done.4.near_ref, bf16[720,256]{1,0:T(8,128)(2,1)S(1)} %get-tuple-element.27.mid_ref, ...), custom_call_target="tpu_custom_call" | custom-call | flops 1604321280 | bytes 2949120 | tf_op jit(solution)/shard_map/pallas_call | solution.py:22
  21.7 0.0 copy-start.1
  21.7 0.0 copy-start.7
  21.7 0.0 copy-start.8
  21.8 0.8 collective-permute-start.7
  22.6 4.0 %collective-permute-start.6 = (bf16[720,256]{1,0:T(8,128)(2,1)S(1)}, bf16[720,256]{1,0:T(8,128)(2,1)S(1)}, u32[]{:S(2)}, u32[]{:S(2)}) collective-permute-start(bf16[720,256]{1,0:T(8,128)(2,1)S(1)} %get-tuple-element.30.mid_ref), channel_id=1, source_target_pairs={{0,16},{32,48},{64,80},{96,112},{128,144},{160,176},{192,208},{224... | collective-permute-start | bytes 1105928 | tf_op jit(solution)/shard_map/ppermute | solution.py:238
  26.6 0.0 collective-permute-done.1.far_ref
  26.6 0.0 collective-permute-done.near_ref
  26.6 3.0 %shard_map.93 = (bf16[720,256]{1,0:T(8,128)(2,1)S(1)}, bf16[720,256]{1,0:T(8,128)(2,1)S(1)}) custom-call(s32[1]{0:T(128)} %bitcast.odd_ref, bf16[2,1,720,256]{3,2,1,0:T(8,128)(2,1)S(1)} %copy-done.3, bf16[720,256]{1,0:T(8,128)(2,1)S(1)} %collective-permute-done.near_ref, bf16[720,256]{1,0:T(8,128)(2,1)S(1)} %get-tuple-element.21.mid_ref, ...), custom_call_target="tpu_custom_call" | custom-call | flops 1604321280 | bytes 2949120 | tf_op jit(solution)/shard_map/pallas_call | solution.py:22
  29.6 0.7 collective-permute-start.3
  30.3 3.2 %collective-permute-start.2 = (bf16[720,256]{1,0:T(8,128)(2,1)S(1)}, bf16[720,256]{1,0:T(8,128)(2,1)S(1)}, u32[]{:S(2)}, u32[]{:S(2)}) collective-permute-start(bf16[720,256]{1,0:T(8,128)(2,1)S(1)} %get-tuple-element.26.mid_ref), channel_id=1, source_target_pairs={{0,16},{32,48},{64,80},{96,112},{128,144},{160,176},{192,208},{224... | collective-permute-start | bytes 1105928 | tf_op jit(solution)/shard_map/ppermute | solution.py:238
  33.6 0.0 collective-permute-done.7.far_ref
  33.6 0.0 collective-permute-done.6.near_ref
  33.6 0.0 copy-done.1
  33.6 0.0 copy-done.7
  33.6 0.0 copy-done.8
  33.6 3.4 %shard_map.95 = (bf16[16,48,256]{2,1,0:T(8,128)(2,1)S(1)}, f32[4,256]{1,0:T(4,128)S(1)}) custom-call(s32[1]{0:T(128)} %bitcast.odd_ref, bf16[720,256]{1,0:T(8,128)(2,1)S(1)} %get-tuple-element.29.x_ref, bf16[720,256]{1,0:T(8,128)(2,1)S(1)} %collective-permute-done.6.near_ref, bf16[720,256]{1,0:T(8,128)(2,1)S(1)} %get-tuple-element.30.mid_ref, ...), custom_call_target="tpu_custom_call" | custom-call | flops 1604321280 | bytes 2949120 | tf_op jit(solution)/shard_map/pallas_call | solution.py:22
  37.0 0.0 collective-permute-done.3.far_ref
  37.0 3.3 %collective-permute-done.2.near_ref = bf16[720,256]{1,0:T(8,128)(2,1)S(1)} collective-permute-done((bf16[720,256]{1,0:T(8,128)(2,1)S(1)}, bf16[720,256]{1,0:T(8,128)(2,1)S(1)}, u32[]{:S(2)}, u32[]{:S(2)}) %collective-permute-start.2) | collective-permute-done | bytes 368672 | tf_op jit(solution)/shard_map/ppermute | solution.py:238
  40.3 0.0 copy-start.9
  40.3 0.0 copy-start.10
  40.3 4.2 %shard_map.96 = (bf16[16,96,256]{2,1,0:T(8,128)(2,1)}, bf16[16,8,256]{2,1,0:T(8,128)(2,1)S(1)}) custom-call(s32[1]{0:T(128)} %bitcast.odd_ref, bf16[720,256]{1,0:T(8,128)(2,1)S(1)} %get-tuple-element.25.x_ref, bf16[720,256]{1,0:T(8,128)(2,1)S(1)} %collective-permute-done.2.near_ref, bf16[720,256]{1,0:T(8,128)(2,1)S(1)} %get-tuple-element.26.mid_ref, ...), custom_call_target="tpu_custom_call" | custom-call | flops 1604321280 | bytes 2949120 | tf_op jit(solution)/shard_map/pallas_call | solution.py:22
  44.5 19.8 %all_to_all.15.seen_ref = bf16[16,8,256]{2,1,0:T(8,128)(2,1)S(1)} all-to-all(bf16[16,8,256]{2,1,0:T(8,128)(2,1)S(1)} %get-tuple-element.34), channel_id=1, replica_groups=mesh['lat'=16,'mem'=16] {'mem'}, dimensions={0} | all-to-all | bytes 131072 | tf_op jit(solution)/shard_map/all_to_all | solution.py:287
  64.3 3.6 %all-to-all-start.1 = ((bf16[16,96,256]{2,1,0:T(8,128)(2,1)}), bf16[16,96,256]{2,1,0:T(8,128)(2,1)S(1)}, u32[]{:S(2)}, u32[]{:S(2)}) async-start(bf16[16,96,256]{2,1,0:T(8,128)(2,1)} %get-tuple-element.36), calls=%async_computation.1 | async-start | bytes 1572864 | tf_op jit(solution)/shard_map/all_to_all | solution.py:289
  67.9 0.0 copy-done.9
  67.9 0.0 copy-done.10
  68.0 0.8 shard_map.97
  68.7 3.0 %collective-permute-start.10 = (f32[32,128]{1,0:T(8,128)S(1)}, f32[32,128]{1,0:T(8,128)S(1)}, u32[]{:S(2)}, u32[]{:S(2)}) collective-permute-start(f32[32,128]{1,0:T(8,128)S(1)} %shard_map.97), channel_id=1, source_target_pairs={{0,48},{16,32},{32,16},{48,0},{64,112},{80,96},{96,80},{112,64},{1... | collective-permute-start | bytes 49160 | tf_op jit(solution)/shard_map/ppermute | solution.py:293
  71.8 0.2 collective-permute-start.9
  72.0 0.4 collective-permute-start.8
  72.4 0.5 collective-permute-done.10
  72.9 3.3 %collective-permute-done.9 = f32[32,128]{1,0:T(8,128)S(1)} collective-permute-done((f32[32,128]{1,0:T(8,128)S(1)}, f32[32,128]{1,0:T(8,128)S(1)}, u32[]{:S(2)}, u32[]{:S(2)}) %collective-permute-start.9) | collective-permute-done | bytes 16416 | tf_op jit(solution)/shard_map/ppermute | solution.py:293
  76.1 0.0 collective-permute-done.8
  76.2 1.2 %collective-permute-start.13 = (f32[32,128]{1,0:T(8,128)S(1)}, f32[32,128]{1,0:T(8,128)S(1)}, u32[]{:S(2)}, u32[]{:S(2)}) collective-permute-start(f32[32,128]{1,0:T(8,128)S(1)} %add_add_fusion.a_ref), channel_id=1, source_target_pairs={{0,192},{16,208},{32,224},{48,240},{64,128},{80,144},{96,160},{112... | collective-permute-start | bytes 49160 | tf_op jit(solution)/shard_map/ppermute | solution.py:293
  77.4 1.9 %collective-permute-start.12 = (f32[32,128]{1,0:T(8,128)S(1)}, f32[32,128]{1,0:T(8,128)S(1)}, u32[]{:S(2)}, u32[]{:S(2)}) collective-permute-start(f32[32,128]{1,0:T(8,128)S(1)} %add_add_fusion.a_ref), channel_id=1, source_target_pairs={{0,128},{16,144},{32,160},{48,176},{64,192},{80,208},{96,224},{112... | collective-permute-start | bytes 49160 | tf_op jit(solution)/shard_map/ppermute | solution.py:293
  79.2 0.3 collective-permute-start.11
  79.5 0.8 collective-permute-done.13.d_ref
  80.3 1.4 %collective-permute-done.12.c_ref = f32[32,128]{1,0:T(8,128)S(1)} collective-permute-done((f32[32,128]{1,0:T(8,128)S(1)}, f32[32,128]{1,0:T(8,128)S(1)}, u32[]{:S(2)}, u32[]{:S(2)}) %collective-permute-start.12) | collective-permute-done | bytes 16416 | tf_op jit(solution)/shard_map/ppermute | solution.py:293
  81.7 0.4 collective-permute-done.11.b_ref
  82.1 2.5 %shard_map.98.weight_ref = bf16[32,32]{1,0:T(8,128)(2,1)S(1)} custom-call(f32[32,128]{1,0:T(8,128)S(1)} %add_add_fusion.a_ref, f32[32,128]{1,0:T(8,128)S(1)} %collective-permute-done.11.b_ref, f32[32,128]{1,0:T(8,128)S(1)} %collective-permute-done.12.c_ref, f32[32,128]{1,0:T(8,128)S(1)} %collective-permute-done.13.d_ref), custom_call_target="tpu_custom_call" | custom-call | tf_op jit(solution)/shard_map/pallas_call | solution.py:22
  84.6 6.0 %all-to-all-done.1.share_ref = bf16[16,96,256]{2,1,0:T(8,128)(2,1)S(1)} async-done(((bf16[16,96,256]{2,1,0:T(8,128)(2,1)}), bf16[16,96,256]{2,1,0:T(8,128)(2,1)S(1)}, u32[]{:S(2)}, u32[]{:S(2)}) %all-to-all-start.1) | async-done | bytes 786464 | tf_op jit(solution)/shard_map/all_to_all | solution.py:289
  90.6 0.8 shard_map.99
  91.5 26.5 %all_to_all.16.in_ref = bf16[16,2,48,256]{3,2,1,0:T(8,128)(2,1)S(1)} all-to-all(bf16[16,2,48,256]{3,2,1,0:T(8,128)(2,1)S(1)} %bitcast.4), channel_id=1, replica_groups=mesh['lat'=16,'mem'=16] {'mem'}, dimensions={0} | all-to-all | bytes 1572864 | tf_op jit(solution)/shard_map/all_to_all | solution.py:305
  118.0 0.9 shard_map.100
  (3 shorter events, 0.0 us)
Async XLA Ops:
  0.0 1.1 copy-start.2
  1.1 0.7 copy-start.5
  1.8 15.2 %copy-start.6 = (f32[2,256]{1,0:T(2,128)S(1)}, f32[2,256]{1,0:T(2,128)}, u32[]{:S(2)}) copy-start(f32[2,256]{1,0:T(2,128)} %rest_0_.3) | copy-start | bytes 6148
  2.1 14.9 %copy-start.3 = (bf16[2,1,720,256]{3,2,1,0:T(8,128)(2,1)S(1)}, bf16[2,1,720,256]{3,2,1,0:T(8,128)(2,1)}, u32[]{:S(2)}) copy-start(bf16[2,1,720,256]{3,2,1,0:T(8,128)(2,1)} %x_ref.5) | copy-start | bytes 2211844
  2.1 14.9 %collective-permute-start.5 = (bf16[720,256]{1,0:T(8,128)(2,1)S(1)}, bf16[720,256]{1,0:T(8,128)(2,1)S(1)}, u32[]{:S(2)}, u32[]{:S(2)}) collective-permute-start(bf16[720,256]{1,0:T(8,128)(2,1)S(1)} %get-tuple-element.27.mid_ref), channel_id=1, source_target_pairs={{16,32},{48,64},{80,96},{112,128},{144,160},{176,192},{208,224},{3... | collective-permute-start | bytes 1105928 | tf_op jit(solution)/shard_map/ppermute | solution.py:238
  3.0 14.0 %collective-permute-start.4 = (bf16[720,256]{1,0:T(8,128)(2,1)S(1)}, bf16[720,256]{1,0:T(8,128)(2,1)S(1)}, u32[]{:S(2)}, u32[]{:S(2)}) collective-permute-start(bf16[720,256]{1,0:T(8,128)(2,1)S(1)} %get-tuple-element.27.mid_ref), channel_id=1, source_target_pairs={{0,16},{32,48},{64,80},{96,112},{128,144},{160,176},{192,208},{224... | collective-permute-start | bytes 1105928 | tf_op jit(solution)/shard_map/ppermute | solution.py:238
  7.7 18.9 %collective-permute-start.1 = (bf16[720,256]{1,0:T(8,128)(2,1)S(1)}, bf16[720,256]{1,0:T(8,128)(2,1)S(1)}, u32[]{:S(2)}, u32[]{:S(2)}) collective-permute-start(bf16[720,256]{1,0:T(8,128)(2,1)S(1)} %get-tuple-element.21.mid_ref), channel_id=1, source_target_pairs={{16,32},{48,64},{80,96},{112,128},{144,160},{176,192},{208,224},{3... | collective-permute-start | bytes 1105928 | tf_op jit(solution)/shard_map/ppermute | solution.py:238
  8.4 18.2 %collective-permute-start = (bf16[720,256]{1,0:T(8,128)(2,1)S(1)}, bf16[720,256]{1,0:T(8,128)(2,1)S(1)}, u32[]{:S(2)}, u32[]{:S(2)}) collective-permute-start(bf16[720,256]{1,0:T(8,128)(2,1)S(1)} %get-tuple-element.21.mid_ref), channel_id=1, source_target_pairs={{0,16},{32,48},{64,80},{96,112},{128,144},{160,176},{192,208},{224... | collective-permute-start | bytes 1105928 | tf_op jit(solution)/shard_map/ppermute | solution.py:238
  11.6 1.2 %copy-start.4 = (bf16[2,256,1024]{2,1,0:T(8,128)(2,1)S(1)}, bf16[2,256,1024]{2,1,0:T(8,128)(2,1)}, u32[]{:S(2)}) copy-start(bf16[2,256,1024]{2,1,0:T(8,128)(2,1)} %refs_1_.1) | copy-start | bytes 3145732
  17.0 1.7 %copy-start = (bf16[2,2304,256]{2,1,0:T(8,128)(2,1)S(1)}, bf16[2,2304,256]{2,1,0:T(8,128)(2,1)}, u32[]{:S(2)}) copy-start(bf16[2,2304,256]{2,1,0:T(8,128)(2,1)} %get-tuple-element.22.conv_ref) | copy-start | bytes 7077892
  21.7 11.9 %copy-start.1 = (bf16[2,2304,256]{2,1,0:T(8,128)(2,1)S(1)}, bf16[2,2304,256]{2,1,0:T(8,128)(2,1)}, u32[]{:S(2)}) copy-start(bf16[2,2304,256]{2,1,0:T(8,128)(2,1)} %get-tuple-element.22.conv_ref) | copy-start | bytes 7077892
  21.7 11.9 %copy-start.7 = (s32[1024]{0:T(1024)S(1)}, s32[1024]{0:T(1024)}, u32[]{:S(2)}) copy-start(s32[1024]{0:T(1024)} %param.14) | copy-start | bytes 12292
  21.7 11.9 %copy-start.8 = (s32[1024]{0:T(1024)S(1)}, s32[1024]{0:T(1024)}, u32[]{:S(2)}) copy-start(s32[1024]{0:T(1024)} %param.15) | copy-start | bytes 12292
  21.8 11.8 %collective-permute-start.7 = (bf16[720,256]{1,0:T(8,128)(2,1)S(1)}, bf16[720,256]{1,0:T(8,128)(2,1)S(1)}, u32[]{:S(2)}, u32[]{:S(2)}) collective-permute-start(bf16[720,256]{1,0:T(8,128)(2,1)S(1)} %get-tuple-element.30.mid_ref), channel_id=1, source_target_pairs={{16,32},{48,64},{80,96},{112,128},{144,160},{176,192},{208,224},{3... | collective-permute-start | bytes 1105928 | tf_op jit(solution)/shard_map/ppermute | solution.py:238
  22.6 11.0 %collective-permute-start.6 = (bf16[720,256]{1,0:T(8,128)(2,1)S(1)}, bf16[720,256]{1,0:T(8,128)(2,1)S(1)}, u32[]{:S(2)}, u32[]{:S(2)}) collective-permute-start(bf16[720,256]{1,0:T(8,128)(2,1)S(1)} %get-tuple-element.30.mid_ref), channel_id=1, source_target_pairs={{0,16},{32,48},{64,80},{96,112},{128,144},{160,176},{192,208},{224... | collective-permute-start | bytes 1105928 | tf_op jit(solution)/shard_map/ppermute | solution.py:238
  29.6 7.3 %collective-permute-start.3 = (bf16[720,256]{1,0:T(8,128)(2,1)S(1)}, bf16[720,256]{1,0:T(8,128)(2,1)S(1)}, u32[]{:S(2)}, u32[]{:S(2)}) collective-permute-start(bf16[720,256]{1,0:T(8,128)(2,1)S(1)} %get-tuple-element.26.mid_ref), channel_id=1, source_target_pairs={{16,32},{48,64},{80,96},{112,128},{144,160},{176,192},{208,224},{3... | collective-permute-start | bytes 1105928 | tf_op jit(solution)/shard_map/ppermute | solution.py:238
  30.3 10.0 %collective-permute-start.2 = (bf16[720,256]{1,0:T(8,128)(2,1)S(1)}, bf16[720,256]{1,0:T(8,128)(2,1)S(1)}, u32[]{:S(2)}, u32[]{:S(2)}) collective-permute-start(bf16[720,256]{1,0:T(8,128)(2,1)S(1)} %get-tuple-element.26.mid_ref), channel_id=1, source_target_pairs={{0,16},{32,48},{64,80},{96,112},{128,144},{160,176},{192,208},{224... | collective-permute-start | bytes 1105928 | tf_op jit(solution)/shard_map/ppermute | solution.py:238
  40.3 27.6 %copy-start.9 = (f32[1024]{0:T(1024)S(1)}, f32[1024]{0:T(1024)}, u32[]{:S(2)}) copy-start(f32[1024]{0:T(1024)} %param.16) | copy-start | bytes 12292
  40.3 27.6 %copy-start.10 = (f32[1024]{0:T(1024)S(1)}, f32[1024]{0:T(1024)}, u32[]{:S(2)}) copy-start(f32[1024]{0:T(1024)} %param.17) | copy-start | bytes 12292
  64.3 26.3 %all-to-all-start.1 = ((bf16[16,96,256]{2,1,0:T(8,128)(2,1)}), bf16[16,96,256]{2,1,0:T(8,128)(2,1)S(1)}, u32[]{:S(2)}, u32[]{:S(2)}) async-start(bf16[16,96,256]{2,1,0:T(8,128)(2,1)} %get-tuple-element.36), calls=%async_computation.1 | async-start | bytes 1572864 | tf_op jit(solution)/shard_map/all_to_all | solution.py:289
  68.7 4.1 %collective-permute-start.10 = (f32[32,128]{1,0:T(8,128)S(1)}, f32[32,128]{1,0:T(8,128)S(1)}, u32[]{:S(2)}, u32[]{:S(2)}) collective-permute-start(f32[32,128]{1,0:T(8,128)S(1)} %shard_map.97), channel_id=1, source_target_pairs={{0,48},{16,32},{32,16},{48,0},{64,112},{80,96},{96,80},{112,64},{1... | collective-permute-start | bytes 49160 | tf_op jit(solution)/shard_map/ppermute | solution.py:293
  71.8 4.4 %collective-permute-start.9 = (f32[32,128]{1,0:T(8,128)S(1)}, f32[32,128]{1,0:T(8,128)S(1)}, u32[]{:S(2)}, u32[]{:S(2)}) collective-permute-start(f32[32,128]{1,0:T(8,128)S(1)} %shard_map.97), channel_id=1, source_target_pairs={{0,32},{16,48},{32,0},{48,16},{64,96},{80,112},{96,64},{112,80},{1... | collective-permute-start | bytes 49160 | tf_op jit(solution)/shard_map/ppermute | solution.py:293
  72.0 4.1 %collective-permute-start.8 = (f32[32,128]{1,0:T(8,128)S(1)}, f32[32,128]{1,0:T(8,128)S(1)}, u32[]{:S(2)}, u32[]{:S(2)}) collective-permute-start(f32[32,128]{1,0:T(8,128)S(1)} %shard_map.97), channel_id=1, source_target_pairs={{0,16},{16,0},{32,48},{48,32},{64,80},{80,64},{96,112},{112,96},{1... | collective-permute-start | bytes 49160 | tf_op jit(solution)/shard_map/ppermute | solution.py:293
  76.2 4.2 %collective-permute-start.13 = (f32[32,128]{1,0:T(8,128)S(1)}, f32[32,128]{1,0:T(8,128)S(1)}, u32[]{:S(2)}, u32[]{:S(2)}) collective-permute-start(f32[32,128]{1,0:T(8,128)S(1)} %add_add_fusion.a_ref), channel_id=1, source_target_pairs={{0,192},{16,208},{32,224},{48,240},{64,128},{80,144},{96,160},{112... | collective-permute-start | bytes 49160 | tf_op jit(solution)/shard_map/ppermute | solution.py:293
  77.4 4.4 %collective-permute-start.12 = (f32[32,128]{1,0:T(8,128)S(1)}, f32[32,128]{1,0:T(8,128)S(1)}, u32[]{:S(2)}, u32[]{:S(2)}) collective-permute-start(f32[32,128]{1,0:T(8,128)S(1)} %add_add_fusion.a_ref), channel_id=1, source_target_pairs={{0,128},{16,144},{32,160},{48,176},{64,192},{80,208},{96,224},{112... | collective-permute-start | bytes 49160 | tf_op jit(solution)/shard_map/ppermute | solution.py:293
  79.2 2.9 %collective-permute-start.11 = (f32[32,128]{1,0:T(8,128)S(1)}, f32[32,128]{1,0:T(8,128)S(1)}, u32[]{:S(2)}, u32[]{:S(2)}) collective-permute-start(f32[32,128]{1,0:T(8,128)S(1)} %add_add_fusion.a_ref), channel_id=1, source_target_pairs={{0,64},{16,80},{32,96},{48,112},{64,0},{80,16},{96,32},{112,48},{1... | collective-permute-start | bytes 49160 | tf_op jit(solution)/shard_map/ppermute | solution.py:293

commit v3 on v2

--- a/solution.py
+++ b/solution.py
@@ -40,23 +40,32 @@
     return (wide * factor * gain).astype(BF16)
 
 
-def first_norm(x_ref, gain_ref, *unit_refs):
-    for m, ref in enumerate(unit_refs):
-        ref[...] = normed(x_ref[m, 0].astype(F32), gain_ref[0:1, :])
-
-
-def load_body(*refs):
+def open_body(latent_ref, gain_in_ref, *refs):
+    *refs, sems = refs
+    gain_ref, refs = refs[0], refs[1:]
+    members = len(refs) // 2
+    copies = [pltpu.make_async_copy(gain_in_ref, gain_ref, sems.at[members])]
+    for m in range(members):
+        copies.append(pltpu.make_async_copy(latent_ref.at[m, 0], refs[m], sems.at[m]))
+    for copy in copies:
+        copy.start()
+    copies[0].wait()
+    for m in range(members):
+        copies[m + 1].wait()
+        refs[members + m][...] = normed(refs[m][...].astype(F32), gain_ref[0:1, :])
+
+
+def load_body(b, *refs):
     sems, refs = refs[-1], refs[:-1]
     count = len(refs) // 2
     copies = []
     for ref, into in zip(refs[:count], refs[count:]):
         rows = ref.shape[1] // 4
-        for b in range(ref.shape[0]):
-            for i in range(4):
-                part = pl.ds(i * rows, rows)
-                copies.append(
-                    pltpu.make_async_copy(ref.at[b, part], into.at[b, part], sems.at[len(copies)])
-                )
+        for i in range(4):
+            part = pl.ds(i * rows, rows)
+            copies.append(
+                pltpu.make_async_copy(ref.at[b, part], into.at[part], sems.at[len(copies)])
+            )
     for copy in copies:
         copy.start()
     for copy in copies:
@@ -78,7 +87,7 @@
     parts = []
     for q in range(3):
         taps = [
-            conv_ref[b, pl.ds(pl.multiple_of((p * 3 + q) * ch, ch), ch), :] for p in lines
+            conv_ref[pl.ds(pl.multiple_of((p * 3 + q) * ch, ch), ch), :] for p in lines
         ]
         parts.append(jnp.dot(rows, jnp.concatenate(taps, axis=0), preferred_element_type=F32))
     mixed[...] = (
@@ -87,8 +96,8 @@
     step = 144
     for start in range(0, lon, step):
         part = pl.ds(start, step)
-        hidden = jax.nn.gelu(jnp.dot(mixed[part, :], up_ref[b], preferred_element_type=F32))
-        branch = jnp.dot(hidden.astype(BF16), down_ref[b], preferred_element_type=F32)
+        hidden = jax.nn.gelu(jnp.dot(mixed[part, :], up_ref[...], preferred_element_type=F32))
+        branch = jnp.dot(hidden.astype(BF16), down_ref[...], preferred_element_type=F32)
         fields = (x_ref[part, :].astype(F32) + branch).astype(BF16)
         fields_ref[part, :] = fields
         if not last:
@@ -227,7 +236,6 @@
     mem = lax.axis_size("mem")
     cell, chan = (v.reshape(1, count) for v in (obs_cell, obs_chan))
     value, var = (v.reshape(count // ch, ch) for v in (obs_value, obs_var))
-    held = [pltpu.VMEM((lon, ch), BF16)]
     odd_row = (lax.axis_index("lat") % 2).reshape(1)
     work = 2 * lon * (9 * ch * ch + 2 * ch * up.shape[2])
     row = shaped((lon, ch), BF16)
@@ -237,52 +245,60 @@
         pairs = [[(i, i + 1) for i in range(start, lat - 1, 2)] for start in (0, 1)]
         return [lax.ppermute(unit, "lat", p + [(j, i) for i, j in p]) for p in pairs]
 
-    def block(b, m, x, near, mid, far, extra, outs, x_spec, halo_spec, scratch=()):
+    def block(b, m, x, near, mid, far, held, extra, outs, scratch=()):
+        args = (odd_row, x, near, mid, far, *held, *extra)
         return call(
             functools.partial(block_body, b, m),
             outs,
-            (odd_row, x, near, mid, far, *held_weights, *extra),
-            [SMEM, x_spec, halo_spec, halo_spec, halo_spec] + [VMEM] * (3 + len(extra)),
-            grid=(1,),
-            scratch=[*scratch, *held],
+            args,
+            [SMEM] + [VMEM] * (len(args) - 1),
+            scratch=[*scratch, pltpu.VMEM((lon, ch), BF16)],
             mib=32,
             flops=work,
             nbytes=8 * lon * ch * 2,
         )
 
-    def latent_spec(m):
-        return pl.BlockSpec((None, None, lon, ch), lambda i: (m, 0, 0, 0))
-
-    units = call(first_norm, (row,) * members, (latent, gains), nbytes=8 * lon * ch)
-    firsts = [(unit, *halo(unit)) for unit in units]
+    def load(b, weights):
+        return call(
+            functools.partial(load_body, b),
+            tuple(shaped(w.shape[1:], BF16) for w in weights),
+            weights,
+            [HBM] * 3,
+            scratch=[pltpu.SemaphoreType.DMA((12,))],
+            mib=48,
+            nbytes=sum(w.size for w in weights),
+        )
+
+    gains, *rows = call(
+        open_body,
+        (shaped(gains.shape, F32),) + (row,) * (2 * members),
+        (latent, gains),
+        [HBM] * 2,
+        scratch=[pltpu.SemaphoreType.DMA((members + 1,))],
+        mib=52,
+        nbytes=8 * lon * ch,
+    )
+    firsts = [(unit, *halo(unit)) for unit in rows[members:]]
     weights = (conv, up, down)
-    held_weights = call(
-        load_body,
-        tuple(shaped(w.shape, BF16) for w in weights),
-        weights,
-        [HBM] * 3,
-        scratch=[pltpu.SemaphoreType.DMA((24,))],
-        mib=50,
-        nbytes=sum(2 * w.size for w in weights),
-    )
+    held = load(0, weights)
     fields, lasts = [], []
     for m, (unit, near, far) in enumerate(firsts):
-        out, unit = block(
-            0, m, latent, near, unit, far, (gains,), (row, row), latent_spec(m), VMEM
-        )
+        out, unit = block(0, m, rows[m], near, unit, far, held, (gains,), (row, row))
         fields.append(out)
         lasts.append((unit, *halo(unit)))
+    weights, _ = lax.optimization_barrier((weights, lasts[1][0]))
+    held = load(1, weights)
     plain = shaped((mem, cells, ch), BF16)
     both = shaped((mem, members * cells, ch), BF16)
     store = [pltpu.VMEM((mem * cells, ch), BF16)]
     fields[0], _ = lax.optimization_barrier((fields[0], lasts[1][0]))
     unit, near, far = lasts[0]
     outs = (plain, shaped((count // ch, ch), F32))
-    even, seen = block(1, 0, fields[0], near, unit, far, (cell, chan), outs, VMEM, VMEM, store)
+    even, seen = block(1, 0, fields[0], near, unit, far, held, (cell, chan), outs, store)
     unit, near, far = lasts[1]
     outs = (both, shaped((mem, 8, ch), BF16))
     share, seen = block(
-        1, 1, fields[1], near, unit, far, (cell, chan, even, seen), outs, VMEM, VMEM, store
+        1, 1, fields[1], near, unit, far, held, (cell, chan, even, seen), outs, store
     )
     seen = lax.all_to_all(seen, "mem", 0, 0, tiled=True)
     share, seen = lax.optimization_barrier((share, seen))

time: 119 us -> 119 us (level)
  waiting for transfers between devices: 15.7 us -> 7.26 us
  blocking collectives: 46.4 us -> 51.9 us
  starting transfers between devices: 28.7 us -> 32.8 us
  local copies, waits for them, and re-layouts: 4.73 us -> 3.16 us
    ppermute x6, starting transfers between devices: 7.01 us -> 12.2 us  [swap(): lax.ppermute(v, axis, [(i, i ^ s) for i in range(size)])]
    all_to_all x1, waiting for transfers between devices: 6.03 us -> 1.03 us  [body(): share = lax.all_to_all(share, 'mem', 0, 0, tiled=True)]
    all_to_all x1, blocking collectives: 26.5 us -> 31.5 us  [body(): lax.all_to_all(mixed.reshape(mem, members, cells, ch), 'mem', 0, 0, tiled...]
    ppermute x8, waiting for transfers between devices: 3.35 us -> 0.02 us  [halo(): lax.ppermute(unit, 'lat', p + [(j, i) for i, j in p])]
    unnamed x22 -> x14, local copies, waits for them, and re-layouts: 4.71 us -> 3.15 us
    pallas_call x10 -> x11, Pallas kernels: 23.1 us -> 22.9 us  [call(): pl.pallas_call(body, out_shape=out_shape, in_specs=specs or [VMEM] * len(...]
  transfers between devices with their start and end apart: 15 -> 15, of which waited for: 7 -> 6; matrix products, arithmetic and copies ran while one was open for 0% -> 0% of each run, Pallas kernels for 14% -> 13%
where the time goes in v3:
time: 119 us; the launch traced here: 118 us
  blocking collectives  51.9 us (44%)
  starting transfers between devices  32.8 us (28%)
  Pallas kernels  22.9 us (19%)
  waiting for transfers between devices  7.26 us (6%)
  local copies, waits for them, and re-layouts  3.16 us (3%)
    all_to_all x1, blocking collectives, body(): lax.all_to_all(mixed.reshape(mem, members, cells, ch), 'mem', 0, 0, tiled...  31.5 us
    pallas_call x11, Pallas kernels, call(): pl.pallas_call(body, out_shape=out_shape, in_specs=specs or [VMEM] * len(...  22.9 us
    all_to_all x1, blocking collectives, body(): seen = lax.all_to_all(seen, 'mem', 0, 0, tiled=True)  20.4 us
    ppermute x8, starting transfers between devices, halo(): lax.ppermute(unit, 'lat', p + [(j, i) for i, j in p])  17.1 us
    ppermute x6, starting transfers between devices, swap(): lax.ppermute(v, axis, [(i, i ^ s) for i in range(size)])  12.2 us
    ppermute x6, waiting for transfers between devices, swap(): lax.ppermute(v, axis, [(i, i ^ s) for i in range(size)])  6.21 us
    all_to_all x1, starting transfers between devices, body(): share = lax.all_to_all(share, 'mem', 0, 0, tiled=True)  3.56 us
    unnamed x14, local copies, waits for them, and re-layouts  3.15 us
  transfers between devices with their start and end apart: 15, of which 6 were waited for; matrix products, arithmetic and copies ran while one was open for 0% of the time, Pallas kernels for 13%

profile of v3, /device:TPU:1, one launch (start us, length us, event | category | flops | bytes accessed | tf_op | source)
XLA Modules:
  0.0 118.2 jit_solution(2723273678045288638)
XLA Ops:
  0.0 0.0 copy-start.2
  0.0 0.7 copy-done.2
  0.7 1.4 %shard_map.91 = (f32[2,256]{1,0:T(2,128)S(1)}, bf16[720,256]{1,0:T(8,128)(2,1)S(1)}, bf16[720,256]{1,0:T(8,128)(2,1)S(1)}, bf16[720,256]{1,0:T(8,128)(2,1)S(1)}, bf16[720,256]{1,0:T(8,128)(2,1)S(1)}) custom-call(bf16[2,1,720,256]{3,2,1,0:T(8,128)(2,1)} %latent_ref.1, f32[2,256]{1,0:T(2,128)S(1)} %copy-done.2), custom_call_target="tpu_custom_call" | custom-call | bytes 1474560 | tf_op jit(solution)/shard_map/pallas_call | solution.py:22
  2.1 2.2 %collective-permute-start.4 = (bf16[720,256]{1,0:T(8,128)(2,1)S(1)}, bf16[720,256]{1,0:T(8,128)(2,1)S(1)}, u32[]{:S(2)}, u32[]{:S(2)}) collective-permute-start(bf16[720,256]{1,0:T(8,128)(2,1)S(1)} %get-tuple-element.45.mid_ref), channel_id=1, source_target_pairs={{0,16},{32,48},{64,80},{96,112},{128,144},{160,176},{192,208},{224... | collective-permute-start | bytes 1105928 | tf_op jit(solution)/shard_map/ppermute | solution.py:246
  4.3 0.7 collective-permute-start.5
  5.0 3.6 %collective-permute-start = (bf16[720,256]{1,0:T(8,128)(2,1)S(1)}, bf16[720,256]{1,0:T(8,128)(2,1)S(1)}, u32[]{:S(2)}, u32[]{:S(2)}) collective-permute-start(bf16[720,256]{1,0:T(8,128)(2,1)S(1)} %get-tuple-element.31.mid_ref), channel_id=1, source_target_pairs={{0,16},{32,48},{64,80},{96,112},{128,144},{160,176},{192,208},{224... | collective-permute-start | bytes 1105928 | tf_op jit(solution)/shard_map/ppermute | solution.py:246
  8.6 0.7 collective-permute-start.1
  9.3 0.0 copy-start
  9.3 1.2 %copy-done = bf16[2,256,1024]{2,1,0:T(8,128)(2,1)S(1)} copy-done((bf16[2,256,1024]{2,1,0:T(8,128)(2,1)S(1)}, bf16[2,256,1024]{2,1,0:T(8,128)(2,1)}, u32[]{:S(2)}) %copy-start) | copy-done | bytes 1048600
  10.5 0.0 copy-start.1
  10.5 1.2 %copy-done.1 = bf16[2,1024,256]{2,1,0:T(8,128)(2,1)S(1)} copy-done((bf16[2,1024,256]{2,1,0:T(8,128)(2,1)S(1)}, bf16[2,1024,256]{2,1,0:T(8,128)(2,1)}, u32[]{:S(2)}) %copy-start.1) | copy-done | bytes 1048600
  11.7 1.5 %shard_map.92 = (bf16[2304,256]{1,0:T(8,128)(2,1)S(1)}, bf16[256,1024]{1,0:T(8,128)(2,1)S(1)}, bf16[1024,256]{1,0:T(8,128)(2,1)S(1)}) custom-call(bf16[2,2304,256]{2,1,0:T(8,128)(2,1)} %refs_0_.2, bf16[2,256,1024]{2,1,0:T(8,128)(2,1)S(1)} %copy-done, bf16[2,1024,256]{2,1,0:T(8,128)(2,1)S(1)} %copy-done.1), custom_call_target="tpu_custom_call" | custom-call | bytes 2228224 | tf_op jit(solution)/shard_map/pallas_call | solution.py:22
  13.2 0.0 collective-permute-done.4.near_ref
  13.2 0.0 collective-permute-done.5.far_ref
  13.2 3.0 %shard_map.95 = (bf16[720,256]{1,0:T(8,128)(2,1)S(1)}, bf16[720,256]{1,0:T(8,128)(2,1)S(1)}) custom-call(s32[1]{0:T(128)} %bitcast.odd_ref, bf16[720,256]{1,0:T(8,128)(2,1)S(1)} %get-tuple-element.44.x_ref, bf16[720,256]{1,0:T(8,128)(2,1)S(1)} %collective-permute-done.4.near_ref, bf16[720,256]{1,0:T(8,128)(2,1)S(1)} %get-tuple-element.45.mid_ref, ...), custom_call_target="tpu_custom_call" | custom-call | flops 1604321280 | bytes 2949120 | tf_op jit(solution)/shard_map/pallas_call | solution.py:22
  16.2 3.5 %collective-permute-start.6 = (bf16[720,256]{1,0:T(8,128)(2,1)S(1)}, bf16[720,256]{1,0:T(8,128)(2,1)S(1)}, u32[]{:S(2)}, u32[]{:S(2)}) collective-permute-start(bf16[720,256]{1,0:T(8,128)(2,1)S(1)} %get-tuple-element.48.mid_ref), channel_id=1, source_target_pairs={{0,16},{32,48},{64,80},{96,112},{128,144},{160,176},{192,208},{224... | collective-permute-start | bytes 1105928 | tf_op jit(solution)/shard_map/ppermute | solution.py:246
  19.7 0.7 collective-permute-start.7
  20.4 0.0 collective-permute-done.near_ref
  20.4 0.0 collective-permute-done.1.far_ref
  20.4 3.0 %shard_map.93 = (bf16[720,256]{1,0:T(8,128)(2,1)S(1)}, bf16[720,256]{1,0:T(8,128)(2,1)S(1)}) custom-call(s32[1]{0:T(128)} %bitcast.odd_ref, bf16[720,256]{1,0:T(8,128)(2,1)S(1)} %get-tuple-element.30.x_ref, bf16[720,256]{1,0:T(8,128)(2,1)S(1)} %collective-permute-done.near_ref, bf16[720,256]{1,0:T(8,128)(2,1)S(1)} %get-tuple-element.31.mid_ref, ...), custom_call_target="tpu_custom_call" | custom-call | flops 1604321280 | bytes 2949120 | tf_op jit(solution)/shard_map/pallas_call | solution.py:22
  23.4 4.9 %collective-permute-start.2 = (bf16[720,256]{1,0:T(8,128)(2,1)S(1)}, bf16[720,256]{1,0:T(8,128)(2,1)S(1)}, u32[]{:S(2)}, u32[]{:S(2)}) collective-permute-start(bf16[720,256]{1,0:T(8,128)(2,1)S(1)} %get-tuple-element.37.mid_ref), channel_id=1, source_target_pairs={{0,16},{32,48},{64,80},{96,112},{128,144},{160,176},{192,208},{224... | collective-permute-start | bytes 1105928 | tf_op jit(solution)/shard_map/ppermute | solution.py:246
  28.3 0.9 collective-permute-start.3
  29.2 0.0 copy-start.3
  29.2 0.0 copy-start.4
  29.2 1.5 %shard_map.94 = (bf16[2304,256]{1,0:T(8,128)(2,1)S(1)}, bf16[256,1024]{1,0:T(8,128)(2,1)S(1)}, bf16[1024,256]{1,0:T(8,128)(2,1)S(1)}) custom-call(bf16[2,2304,256]{2,1,0:T(8,128)(2,1)} %refs_0_.2, bf16[2,256,1024]{2,1,0:T(8,128)(2,1)S(1)} %copy-done, bf16[2,1024,256]{2,1,0:T(8,128)(2,1)S(1)} %copy-done.1), custom_call_target="tpu_custom_call" | custom-call | bytes 2228224 | tf_op jit(solution)/shard_map/pallas_call | solution.py:22
  30.7 0.0 collective-permute-done.6.near_ref
  30.7 0.0 collective-permute-done.7.far_ref
  30.7 0.0 copy-done.3
  30.7 0.0 copy-done.4
  30.7 3.4 %shard_map.96 = (bf16[16,48,256]{2,1,0:T(8,128)(2,1)S(1)}, f32[4,256]{1,0:T(4,128)S(1)}) custom-call(s32[1]{0:T(128)} %bitcast.odd_ref, bf16[720,256]{1,0:T(8,128)(2,1)S(1)} %get-tuple-element.47.x_ref, bf16[720,256]{1,0:T(8,128)(2,1)S(1)} %collective-permute-done.6.near_ref, bf16[720,256]{1,0:T(8,128)(2,1)S(1)} %get-tuple-element.48.mid_ref, ...), custom_call_target="tpu_custom_call" | custom-call | flops 1604321280 | bytes 2949120 | tf_op jit(solution)/shard_map/pallas_call | solution.py:22
  34.1 0.0 collective-permute-done.2.near_ref
  34.1 0.0 collective-permute-done.3.far_ref
  34.1 4.2 %shard_map.97 = (bf16[16,96,256]{2,1,0:T(8,128)(2,1)}, bf16[16,8,256]{2,1,0:T(8,128)(2,1)S(1)}) custom-call(s32[1]{0:T(128)} %bitcast.odd_ref, bf16[720,256]{1,0:T(8,128)(2,1)S(1)} %get-tuple-element.36.x_ref, bf16[720,256]{1,0:T(8,128)(2,1)S(1)} %collective-permute-done.2.near_ref, bf16[720,256]{1,0:T(8,128)(2,1)S(1)} %get-tuple-element.37.mid_ref, ...), custom_call_target="tpu_custom_call" | custom-call | flops 1604321280 | bytes 2949120 | tf_op jit(solution)/shard_map/pallas_call | solution.py:22
  38.3 0.0 copy-start.5
  38.3 0.0 copy-start.6
  38.3 20.4 %all_to_all.15.seen_ref = bf16[16,8,256]{2,1,0:T(8,128)(2,1)S(1)} all-to-all(bf16[16,8,256]{2,1,0:T(8,128)(2,1)S(1)} %get-tuple-element.52), channel_id=1, replica_groups=mesh['lat'=16,'mem'=16] {'mem'}, dimensions={0} | all-to-all | bytes 131072 | tf_op jit(solution)/shard_map/all_to_all | solution.py:303
  58.7 3.6 %all-to-all-start.1 = ((bf16[16,96,256]{2,1,0:T(8,128)(2,1)}), bf16[16,96,256]{2,1,0:T(8,128)(2,1)S(1)}, u32[]{:S(2)}, u32[]{:S(2)}) async-start(bf16[16,96,256]{2,1,0:T(8,128)(2,1)} %get-tuple-element.54), calls=%async_computation.1 | async-start | bytes 1572864 | tf_op jit(solution)/shard_map/all_to_all | solution.py:305
  62.3 0.0 copy-done.5
  62.3 0.0 copy-done.6
  62.3 0.8 shard_map.98
  63.1 7.0 %collective-permute-start.10 = (f32[32,128]{1,0:T(8,128)S(1)}, f32[32,128]{1,0:T(8,128)S(1)}, u32[]{:S(2)}, u32[]{:S(2)}) collective-permute-start(f32[32,128]{1,0:T(8,128)S(1)} %shard_map.98), channel_id=1, source_target_pairs={{0,48},{16,32},{32,16},{48,0},{64,112},{80,96},{96,80},{112,64},{1... | collective-permute-start | bytes 49160 | tf_op jit(solution)/shard_map/ppermute | solution.py:309
  70.2 0.0 collective-permute-start.8
  70.2 1.3 %collective-permute-start.9 = (f32[32,128]{1,0:T(8,128)S(1)}, f32[32,128]{1,0:T(8,128)S(1)}, u32[]{:S(2)}, u32[]{:S(2)}) collective-permute-start(f32[32,128]{1,0:T(8,128)S(1)} %shard_map.98), channel_id=1, source_target_pairs={{0,32},{16,48},{32,0},{48,16},{64,96},{80,112},{96,64},{112,80},{1... | collective-permute-start | bytes 49160 | tf_op jit(solution)/shard_map/ppermute | solution.py:309
  71.4 0.2 collective-permute-done.10
  71.6 1.5 %collective-permute-done.8 = f32[32,128]{1,0:T(8,128)S(1)} collective-permute-done((f32[32,128]{1,0:T(8,128)S(1)}, f32[32,128]{1,0:T(8,128)S(1)}, u32[]{:S(2)}, u32[]{:S(2)}) %collective-permute-start.8) | collective-permute-done | bytes 16416 | tf_op jit(solution)/shard_map/ppermute | solution.py:309
  73.0 1.5 %collective-permute-done.9 = f32[32,128]{1,0:T(8,128)S(1)} collective-permute-done((f32[32,128]{1,0:T(8,128)S(1)}, f32[32,128]{1,0:T(8,128)S(1)}, u32[]{:S(2)}, u32[]{:S(2)}) %collective-permute-start.9) | collective-permute-done | bytes 16416 | tf_op jit(solution)/shard_map/ppermute | solution.py:309
  74.6 1.2 %collective-permute-start.11 = (f32[32,128]{1,0:T(8,128)S(1)}, f32[32,128]{1,0:T(8,128)S(1)}, u32[]{:S(2)}, u32[]{:S(2)}) collective-permute-start(f32[32,128]{1,0:T(8,128)S(1)} %add_add_fusion.a_ref), channel_id=1, source_target_pairs={{0,64},{16,80},{32,96},{48,112},{64,0},{80,16},{96,32},{112,48},{1... | collective-permute-start | bytes 49160 | tf_op jit(solution)/shard_map/ppermute | solution.py:309
  75.8 1.6 %collective-permute-start.12 = (f32[32,128]{1,0:T(8,128)S(1)}, f32[32,128]{1,0:T(8,128)S(1)}, u32[]{:S(2)}, u32[]{:S(2)}) collective-permute-start(f32[32,128]{1,0:T(8,128)S(1)} %add_add_fusion.a_ref), channel_id=1, source_target_pairs={{0,128},{16,144},{32,160},{48,176},{64,192},{80,208},{96,224},{112... | collective-permute-start | bytes 49160 | tf_op jit(solution)/shard_map/ppermute | solution.py:309
  77.4 1.0 collective-permute-start.13
  78.4 0.0 collective-permute-done.11.b_ref
  78.4 1.4 %collective-permute-done.12.c_ref = f32[32,128]{1,0:T(8,128)S(1)} collective-permute-done((f32[32,128]{1,0:T(8,128)S(1)}, f32[32,128]{1,0:T(8,128)S(1)}, u32[]{:S(2)}, u32[]{:S(2)}) %collective-permute-start.12) | collective-permute-done | bytes 16416 | tf_op jit(solution)/shard_map/ppermute | solution.py:309
  79.9 1.6 %collective-permute-done.13.d_ref = f32[32,128]{1,0:T(8,128)S(1)} collective-permute-done((f32[32,128]{1,0:T(8,128)S(1)}, f32[32,128]{1,0:T(8,128)S(1)}, u32[]{:S(2)}, u32[]{:S(2)}) %collective-permute-start.13) | collective-permute-done | bytes 16416 | tf_op jit(solution)/shard_map/ppermute | solution.py:309
  81.5 2.5 %shard_map.99.weight_ref = bf16[32,32]{1,0:T(8,128)(2,1)S(1)} custom-call(f32[32,128]{1,0:T(8,128)S(1)} %add_add_fusion.a_ref, f32[32,128]{1,0:T(8,128)S(1)} %collective-permute-done.11.b_ref, f32[32,128]{1,0:T(8,128)S(1)} %collective-permute-done.12.c_ref, f32[32,128]{1,0:T(8,128)S(1)} %collective-permute-done.13.d_ref), custom_call_target="tpu_custom_call" | custom-call | tf_op jit(solution)/shard_map/pallas_call | solution.py:22
  84.0 1.0 all-to-all-done.1.share_ref
  85.0 0.8 shard_map.100
  85.8 31.5 %all_to_all.16.in_ref = bf16[16,2,48,256]{3,2,1,0:T(8,128)(2,1)S(1)} all-to-all(bf16[16,2,48,256]{3,2,1,0:T(8,128)(2,1)S(1)} %bitcast.4), channel_id=1, replica_groups=mesh['lat'=16,'mem'=16] {'mem'}, dimensions={0} | all-to-all | bytes 1572864 | tf_op jit(solution)/shard_map/all_to_all | solution.py:321
  117.3 0.9 shard_map.101
  (3 shorter events, 0.0 us)
Async XLA Ops:
  0.0 0.7 copy-start.2
  2.1 11.1 %collective-permute-start.4 = (bf16[720,256]{1,0:T(8,128)(2,1)S(1)}, bf16[720,256]{1,0:T(8,128)(2,1)S(1)}, u32[]{:S(2)}, u32[]{:S(2)}) collective-permute-start(bf16[720,256]{1,0:T(8,128)(2,1)S(1)} %get-tuple-element.45.mid_ref), channel_id=1, source_target_pairs={{0,16},{32,48},{64,80},{96,112},{128,144},{160,176},{192,208},{224... | collective-permute-start | bytes 1105928 | tf_op jit(solution)/shard_map/ppermute | solution.py:246
  4.3 8.9 %collective-permute-start.5 = (bf16[720,256]{1,0:T(8,128)(2,1)S(1)}, bf16[720,256]{1,0:T(8,128)(2,1)S(1)}, u32[]{:S(2)}, u32[]{:S(2)}) collective-permute-start(bf16[720,256]{1,0:T(8,128)(2,1)S(1)} %get-tuple-element.45.mid_ref), channel_id=1, source_target_pairs={{16,32},{48,64},{80,96},{112,128},{144,160},{176,192},{208,224},{3... | collective-permute-start | bytes 1105928 | tf_op jit(solution)/shard_map/ppermute | solution.py:246
  5.0 15.4 %collective-permute-start = (bf16[720,256]{1,0:T(8,128)(2,1)S(1)}, bf16[720,256]{1,0:T(8,128)(2,1)S(1)}, u32[]{:S(2)}, u32[]{:S(2)}) collective-permute-start(bf16[720,256]{1,0:T(8,128)(2,1)S(1)} %get-tuple-element.31.mid_ref), channel_id=1, source_target_pairs={{0,16},{32,48},{64,80},{96,112},{128,144},{160,176},{192,208},{224... | collective-permute-start | bytes 1105928 | tf_op jit(solution)/shard_map/ppermute | solution.py:246
  8.6 11.8 %collective-permute-start.1 = (bf16[720,256]{1,0:T(8,128)(2,1)S(1)}, bf16[720,256]{1,0:T(8,128)(2,1)S(1)}, u32[]{:S(2)}, u32[]{:S(2)}) collective-permute-start(bf16[720,256]{1,0:T(8,128)(2,1)S(1)} %get-tuple-element.31.mid_ref), channel_id=1, source_target_pairs={{16,32},{48,64},{80,96},{112,128},{144,160},{176,192},{208,224},{3... | collective-permute-start | bytes 1105928 | tf_op jit(solution)/shard_map/ppermute | solution.py:246
  9.3 1.2 %copy-start = (bf16[2,256,1024]{2,1,0:T(8,128)(2,1)S(1)}, bf16[2,256,1024]{2,1,0:T(8,128)(2,1)}, u32[]{:S(2)}) copy-start(bf16[2,256,1024]{2,1,0:T(8,128)(2,1)} %refs_1_.2) | copy-start | bytes 3145732
  10.5 1.2 %copy-start.1 = (bf16[2,1024,256]{2,1,0:T(8,128)(2,1)S(1)}, bf16[2,1024,256]{2,1,0:T(8,128)(2,1)}, u32[]{:S(2)}) copy-start(bf16[2,1024,256]{2,1,0:T(8,128)(2,1)} %refs_2_.2) | copy-start | bytes 3145732
  16.2 14.5 %collective-permute-start.6 = (bf16[720,256]{1,0:T(8,128)(2,1)S(1)}, bf16[720,256]{1,0:T(8,128)(2,1)S(1)}, u32[]{:S(2)}, u32[]{:S(2)}) collective-permute-start(bf16[720,256]{1,0:T(8,128)(2,1)S(1)} %get-tuple-element.48.mid_ref), channel_id=1, source_target_pairs={{0,16},{32,48},{64,80},{96,112},{128,144},{160,176},{192,208},{224... | collective-permute-start | bytes 1105928 | tf_op jit(solution)/shard_map/ppermute | solution.py:246
  19.7 11.0 %collective-permute-start.7 = (bf16[720,256]{1,0:T(8,128)(2,1)S(1)}, bf16[720,256]{1,0:T(8,128)(2,1)S(1)}, u32[]{:S(2)}, u32[]{:S(2)}) collective-permute-start(bf16[720,256]{1,0:T(8,128)(2,1)S(1)} %get-tuple-element.48.mid_ref), channel_id=1, source_target_pairs={{16,32},{48,64},{80,96},{112,128},{144,160},{176,192},{208,224},{3... | collective-permute-start | bytes 1105928 | tf_op jit(solution)/shard_map/ppermute | solution.py:246
  23.4 10.7 %collective-permute-start.2 = (bf16[720,256]{1,0:T(8,128)(2,1)S(1)}, bf16[720,256]{1,0:T(8,128)(2,1)S(1)}, u32[]{:S(2)}, u32[]{:S(2)}) collective-permute-start(bf16[720,256]{1,0:T(8,128)(2,1)S(1)} %get-tuple-element.37.mid_ref), channel_id=1, source_target_pairs={{0,16},{32,48},{64,80},{96,112},{128,144},{160,176},{192,208},{224... | collective-permute-start | bytes 1105928 | tf_op jit(solution)/shard_map/ppermute | solution.py:246
  28.3 5.8 %collective-permute-start.3 = (bf16[720,256]{1,0:T(8,128)(2,1)S(1)}, bf16[720,256]{1,0:T(8,128)(2,1)S(1)}, u32[]{:S(2)}, u32[]{:S(2)}) collective-permute-start(bf16[720,256]{1,0:T(8,128)(2,1)S(1)} %get-tuple-element.37.mid_ref), channel_id=1, source_target_pairs={{16,32},{48,64},{80,96},{112,128},{144,160},{176,192},{208,224},{3... | collective-permute-start | bytes 1105928 | tf_op jit(solution)/shard_map/ppermute | solution.py:246
  29.2 1.5 %copy-start.3 = (s32[1024]{0:T(1024)S(1)}, s32[1024]{0:T(1024)}, u32[]{:S(2)}) copy-start(s32[1024]{0:T(1024)} %param.14) | copy-start | bytes 12292
  29.2 1.5 %copy-start.4 = (s32[1024]{0:T(1024)S(1)}, s32[1024]{0:T(1024)}, u32[]{:S(2)}) copy-start(s32[1024]{0:T(1024)} %param.15) | copy-start | bytes 12292
  38.3 23.9 %copy-start.5 = (f32[1024]{0:T(1024)S(1)}, f32[1024]{0:T(1024)}, u32[]{:S(2)}) copy-start(f32[1024]{0:T(1024)} %param.16) | copy-start | bytes 12292
  38.3 24.0 %copy-start.6 = (f32[1024]{0:T(1024)S(1)}, f32[1024]{0:T(1024)}, u32[]{:S(2)}) copy-start(f32[1024]{0:T(1024)} %param.17) | copy-start | bytes 12292
  58.7 26.3 %all-to-all-start.1 = ((bf16[16,96,256]{2,1,0:T(8,128)(2,1)}), bf16[16,96,256]{2,1,0:T(8,128)(2,1)S(1)}, u32[]{:S(2)}, u32[]{:S(2)}) async-start(bf16[16,96,256]{2,1,0:T(8,128)(2,1)} %get-tuple-element.54), calls=%async_computation.1 | async-start | bytes 1572864 | tf_op jit(solution)/shard_map/all_to_all | solution.py:305
  63.1 8.5 %collective-permute-start.10 = (f32[32,128]{1,0:T(8,128)S(1)}, f32[32,128]{1,0:T(8,128)S(1)}, u32[]{:S(2)}, u32[]{:S(2)}) collective-permute-start(f32[32,128]{1,0:T(8,128)S(1)} %shard_map.98), channel_id=1, source_target_pairs={{0,48},{16,32},{32,16},{48,0},{64,112},{80,96},{96,80},{112,64},{1... | collective-permute-start | bytes 49160 | tf_op jit(solution)/shard_map/ppermute | solution.py:309
  70.2 2.9 %collective-permute-start.8 = (f32[32,128]{1,0:T(8,128)S(1)}, f32[32,128]{1,0:T(8,128)S(1)}, u32[]{:S(2)}, u32[]{:S(2)}) collective-permute-start(f32[32,128]{1,0:T(8,128)S(1)} %shard_map.98), channel_id=1, source_target_pairs={{0,16},{16,0},{32,48},{48,32},{64,80},{80,64},{96,112},{112,96},{1... | collective-permute-start | bytes 49160 | tf_op jit(solution)/shard_map/ppermute | solution.py:309
  70.2 4.4 %collective-permute-start.9 = (f32[32,128]{1,0:T(8,128)S(1)}, f32[32,128]{1,0:T(8,128)S(1)}, u32[]{:S(2)}, u32[]{:S(2)}) collective-permute-start(f32[32,128]{1,0:T(8,128)S(1)} %shard_map.98), channel_id=1, source_target_pairs={{0,32},{16,48},{32,0},{48,16},{64,96},{80,112},{96,64},{112,80},{1... | collective-permute-start | bytes 49160 | tf_op jit(solution)/shard_map/ppermute | solution.py:309
  74.6 3.9 %collective-permute-start.11 = (f32[32,128]{1,0:T(8,128)S(1)}, f32[32,128]{1,0:T(8,128)S(1)}, u32[]{:S(2)}, u32[]{:S(2)}) collective-permute-start(f32[32,128]{1,0:T(8,128)S(1)} %add_add_fusion.a_ref), channel_id=1, source_target_pairs={{0,64},{16,80},{32,96},{48,112},{64,0},{80,16},{96,32},{112,48},{1... | collective-permute-start | bytes 49160 | tf_op jit(solution)/shard_map/ppermute | solution.py:309
  75.8 4.1 %collective-permute-start.12 = (f32[32,128]{1,0:T(8,128)S(1)}, f32[32,128]{1,0:T(8,128)S(1)}, u32[]{:S(2)}, u32[]{:S(2)}) collective-permute-start(f32[32,128]{1,0:T(8,128)S(1)} %add_add_fusion.a_ref), channel_id=1, source_target_pairs={{0,128},{16,144},{32,160},{48,176},{64,192},{80,208},{96,224},{112... | collective-permute-start | bytes 49160 | tf_op jit(solution)/shard_map/ppermute | solution.py:309
  77.4 4.1 %collective-permute-start.13 = (f32[32,128]{1,0:T(8,128)S(1)}, f32[32,128]{1,0:T(8,128)S(1)}, u32[]{:S(2)}, u32[]{:S(2)}) collective-permute-start(f32[32,128]{1,0:T(8,128)S(1)} %add_add_fusion.a_ref), channel_id=1, source_target_pairs={{0,192},{16,208},{32,224},{48,240},{64,128},{80,144},{96,160},{112... | collective-permute-start | bytes 49160 | tf_op jit(solution)/shard_map/ppermute | solution.py:309

commit v4 on v3

--- a/solution.py
+++ b/solution.py
@@ -221,12 +221,18 @@
             out_ref[i, part, :] = sums[i * group : (i + 1) * group, :]
 
 
-def place_body(in_ref, out_ref):
+def place_body(in_ref, out_ref, sems):
     lon = out_ref.shape[2]
     cells = in_ref.shape[2]
+    copies = []
     for i in range(lon // cells):
         for m in range(out_ref.shape[0]):
-            out_ref[m, 0, i * cells : (i + 1) * cells, :] = in_ref[i, m]
+            into = out_ref.at[m, 0, pl.ds(i * cells, cells)]
+            copies.append(pltpu.make_async_copy(in_ref.at[i, m], into, sems.at[len(copies)]))
+    for copy in copies:
+        copy.start()
+    for copy in copies:
+        copy.wait()
 
 
 def body(latent, gains, conv, up, down, obs_cell, obs_chan, obs_value, obs_var):
@@ -319,7 +325,13 @@
     weights = call(transform_body, shaped((members * mem, members * mem), BF16), sums)
     mixed = call(combine_body, shaped((members * mem, cells, ch), BF16), (weights, share))
     mixed = lax.all_to_all(mixed.reshape(mem, members, cells, ch), "mem", 0, 0, tiled=True)
-    return call(place_body, shaped(latent.shape, BF16), (mixed,))
+    return call(
+        place_body,
+        shaped(latent.shape, BF16),
+        (mixed,),
+        out_specs=HBM,
+        scratch=[pltpu.SemaphoreType.DMA((members * mem,))],
+    )
 
 
 def solution(mesh):

time: 119 us -> 119 us (level)
  no operation moved by 1% of the time
where the time goes in v4:
time: 119 us
  blocking collectives  51.9 us (44%)
  starting transfers between devices  32.8 us (28%)
  Pallas kernels  23.1 us (19%)
  waiting for transfers between devices  7.26 us (6%)
  local copies, waits for them, and re-layouts  3.16 us (3%)
    all_to_all x1, blocking collectives, body(): lax.all_to_all(mixed.reshape(mem, members, cells, ch), 'mem', 0, 0, tiled...  31.5 us
    pallas_call x11, Pallas kernels, call(): pl.pallas_call(body, out_shape=out_shape, in_specs=specs or [VMEM] * len(...  23.1 us
    all_to_all x1, blocking collectives, body(): seen = lax.all_to_all(seen, 'mem', 0, 0, tiled=True)  20.4 us
    ppermute x8, starting transfers between devices, halo(): lax.ppermute(unit, 'lat', p + [(j, i) for i, j in p])  17.1 us
    ppermute x6, starting transfers between devices, swap(): lax.ppermute(v, axis, [(i, i ^ s) for i in range(size)])  12.2 us
    ppermute x6, waiting for transfers between devices, swap(): lax.ppermute(v, axis, [(i, i ^ s) for i in range(size)])  6.21 us
    all_to_all x1, starting transfers between devices, body(): share = lax.all_to_all(share, 'mem', 0, 0, tiled=True)  3.56 us
    unnamed x14, local copies, waits for them, and re-layouts  3.15 us
  transfers between devices with their start and end apart: 15, of which 6 were waited for; matrix products, arithmetic and copies ran while one was open for 0% of the time, Pallas kernels for 13%

profile of v4, /device:TPU:1, one launch (start us, length us, event | category | flops | bytes accessed | tf_op | source)
XLA Modules:
  0.0 118.6 jit_solution(8610121770490070187)
XLA Ops:
  0.0 0.0 copy-start.2
  0.0 0.7 copy-done.2
  0.7 1.4 %shard_map.91 = (f32[2,256]{1,0:T(2,128)S(1)}, bf16[720,256]{1,0:T(8,128)(2,1)S(1)}, bf16[720,256]{1,0:T(8,128)(2,1)S(1)}, bf16[720,256]{1,0:T(8,128)(2,1)S(1)}, bf16[720,256]{1,0:T(8,128)(2,1)S(1)}) custom-call(bf16[2,1,720,256]{3,2,1,0:T(8,128)(2,1)} %latent_ref.1, f32[2,256]{1,0:T(2,128)S(1)} %copy-done.2), custom_call_target="tpu_custom_call" | custom-call | bytes 1474560 | tf_op jit(solution)/shard_map/pallas_call | solution.py:22
  2.1 2.2 %collective-permute-start.4 = (bf16[720,256]{1,0:T(8,128)(2,1)S(1)}, bf16[720,256]{1,0:T(8,128)(2,1)S(1)}, u32[]{:S(2)}, u32[]{:S(2)}) collective-permute-start(bf16[720,256]{1,0:T(8,128)(2,1)S(1)} %get-tuple-element.45.mid_ref), channel_id=1, source_target_pairs={{0,16},{32,48},{64,80},{96,112},{128,144},{160,176},{192,208},{224... | collective-permute-start | bytes 1105928 | tf_op jit(solution)/shard_map/ppermute | solution.py:252
  4.3 0.7 collective-permute-start.5
  5.0 3.6 %collective-permute-start = (bf16[720,256]{1,0:T(8,128)(2,1)S(1)}, bf16[720,256]{1,0:T(8,128)(2,1)S(1)}, u32[]{:S(2)}, u32[]{:S(2)}) collective-permute-start(bf16[720,256]{1,0:T(8,128)(2,1)S(1)} %get-tuple-element.31.mid_ref), channel_id=1, source_target_pairs={{0,16},{32,48},{64,80},{96,112},{128,144},{160,176},{192,208},{224... | collective-permute-start | bytes 1105928 | tf_op jit(solution)/shard_map/ppermute | solution.py:252
  8.6 0.7 collective-permute-start.1
  9.3 0.0 copy-start
  9.3 1.2 %copy-done = bf16[2,256,1024]{2,1,0:T(8,128)(2,1)S(1)} copy-done((bf16[2,256,1024]{2,1,0:T(8,128)(2,1)S(1)}, bf16[2,256,1024]{2,1,0:T(8,128)(2,1)}, u32[]{:S(2)}) %copy-start) | copy-done | bytes 1048600
  10.5 0.0 copy-start.1
  10.5 1.2 %copy-done.1 = bf16[2,1024,256]{2,1,0:T(8,128)(2,1)S(1)} copy-done((bf16[2,1024,256]{2,1,0:T(8,128)(2,1)S(1)}, bf16[2,1024,256]{2,1,0:T(8,128)(2,1)}, u32[]{:S(2)}) %copy-start.1) | copy-done | bytes 1048600
  11.7 1.5 %shard_map.92 = (bf16[2304,256]{1,0:T(8,128)(2,1)S(1)}, bf16[256,1024]{1,0:T(8,128)(2,1)S(1)}, bf16[1024,256]{1,0:T(8,128)(2,1)S(1)}) custom-call(bf16[2,2304,256]{2,1,0:T(8,128)(2,1)} %refs_0_.2, bf16[2,256,1024]{2,1,0:T(8,128)(2,1)S(1)} %copy-done, bf16[2,1024,256]{2,1,0:T(8,128)(2,1)S(1)} %copy-done.1), custom_call_target="tpu_custom_call" | custom-call | bytes 2228224 | tf_op jit(solution)/shard_map/pallas_call | solution.py:22
  13.2 0.0 collective-permute-done.4.near_ref
  13.2 0.0 collective-permute-done.5.far_ref
  13.2 3.0 %shard_map.95 = (bf16[720,256]{1,0:T(8,128)(2,1)S(1)}, bf16[720,256]{1,0:T(8,128)(2,1)S(1)}) custom-call(s32[1]{0:T(128)} %bitcast.odd_ref, bf16[720,256]{1,0:T(8,128)(2,1)S(1)} %get-tuple-element.44.x_ref, bf16[720,256]{1,0:T(8,128)(2,1)S(1)} %collective-permute-done.4.near_ref, bf16[720,256]{1,0:T(8,128)(2,1)S(1)} %get-tuple-element.45.mid_ref, ...), custom_call_target="tpu_custom_call" | custom-call | flops 1604321280 | bytes 2949120 | tf_op jit(solution)/shard_map/pallas_call | solution.py:22
  16.2 3.5 %collective-permute-start.6 = (bf16[720,256]{1,0:T(8,128)(2,1)S(1)}, bf16[720,256]{1,0:T(8,128)(2,1)S(1)}, u32[]{:S(2)}, u32[]{:S(2)}) collective-permute-start(bf16[720,256]{1,0:T(8,128)(2,1)S(1)} %get-tuple-element.48.mid_ref), channel_id=1, source_target_pairs={{0,16},{32,48},{64,80},{96,112},{128,144},{160,176},{192,208},{224... | collective-permute-start | bytes 1105928 | tf_op jit(solution)/shard_map/ppermute | solution.py:252
  19.7 0.7 collective-permute-start.7
  20.4 0.0 collective-permute-done.near_ref
  20.4 0.0 collective-permute-done.1.far_ref
  20.4 3.0 %shard_map.93 = (bf16[720,256]{1,0:T(8,128)(2,1)S(1)}, bf16[720,256]{1,0:T(8,128)(2,1)S(1)}) custom-call(s32[1]{0:T(128)} %bitcast.odd_ref, bf16[720,256]{1,0:T(8,128)(2,1)S(1)} %get-tuple-element.30.x_ref, bf16[720,256]{1,0:T(8,128)(2,1)S(1)} %collective-permute-done.near_ref, bf16[720,256]{1,0:T(8,128)(2,1)S(1)} %get-tuple-element.31.mid_ref, ...), custom_call_target="tpu_custom_call" | custom-call | flops 1604321280 | bytes 2949120 | tf_op jit(solution)/shard_map/pallas_call | solution.py:22
  23.4 4.9 %collective-permute-start.2 = (bf16[720,256]{1,0:T(8,128)(2,1)S(1)}, bf16[720,256]{1,0:T(8,128)(2,1)S(1)}, u32[]{:S(2)}, u32[]{:S(2)}) collective-permute-start(bf16[720,256]{1,0:T(8,128)(2,1)S(1)} %get-tuple-element.37.mid_ref), channel_id=1, source_target_pairs={{0,16},{32,48},{64,80},{96,112},{128,144},{160,176},{192,208},{224... | collective-permute-start | bytes 1105928 | tf_op jit(solution)/shard_map/ppermute | solution.py:252
  28.3 0.9 collective-permute-start.3
  29.2 0.0 copy-start.3
  29.2 0.0 copy-start.4
  29.2 1.5 %shard_map.94 = (bf16[2304,256]{1,0:T(8,128)(2,1)S(1)}, bf16[256,1024]{1,0:T(8,128)(2,1)S(1)}, bf16[1024,256]{1,0:T(8,128)(2,1)S(1)}) custom-call(bf16[2,2304,256]{2,1,0:T(8,128)(2,1)} %refs_0_.2, bf16[2,256,1024]{2,1,0:T(8,128)(2,1)S(1)} %copy-done, bf16[2,1024,256]{2,1,0:T(8,128)(2,1)S(1)} %copy-done.1), custom_call_target="tpu_custom_call" | custom-call | bytes 2228224 | tf_op jit(solution)/shard_map/pallas_call | solution.py:22
  30.7 0.0 collective-permute-done.6.near_ref
  30.7 0.0 collective-permute-done.7.far_ref
  30.7 0.0 copy-done.3
  30.7 0.0 copy-done.4
  30.7 3.4 %shard_map.96 = (bf16[16,48,256]{2,1,0:T(8,128)(2,1)S(1)}, f32[4,256]{1,0:T(4,128)S(1)}) custom-call(s32[1]{0:T(128)} %bitcast.odd_ref, bf16[720,256]{1,0:T(8,128)(2,1)S(1)} %get-tuple-element.47.x_ref, bf16[720,256]{1,0:T(8,128)(2,1)S(1)} %collective-permute-done.6.near_ref, bf16[720,256]{1,0:T(8,128)(2,1)S(1)} %get-tuple-element.48.mid_ref, ...), custom_call_target="tpu_custom_call" | custom-call | flops 1604321280 | bytes 2949120 | tf_op jit(solution)/shard_map/pallas_call | solution.py:22
  34.1 0.0 collective-permute-done.2.near_ref
  34.1 0.0 collective-permute-done.3.far_ref
  34.1 4.2 %shard_map.97 = (bf16[16,96,256]{2,1,0:T(8,128)(2,1)}, bf16[16,8,256]{2,1,0:T(8,128)(2,1)S(1)}) custom-call(s32[1]{0:T(128)} %bitcast.odd_ref, bf16[720,256]{1,0:T(8,128)(2,1)S(1)} %get-tuple-element.36.x_ref, bf16[720,256]{1,0:T(8,128)(2,1)S(1)} %collective-permute-done.2.near_ref, bf16[720,256]{1,0:T(8,128)(2,1)S(1)} %get-tuple-element.37.mid_ref, ...), custom_call_target="tpu_custom_call" | custom-call | flops 1604321280 | bytes 2949120 | tf_op jit(solution)/shard_map/pallas_call | solution.py:22
  38.3 0.0 copy-start.5
  38.3 0.0 copy-start.6
  38.3 20.4 %all_to_all.15.seen_ref = bf16[16,8,256]{2,1,0:T(8,128)(2,1)S(1)} all-to-all(bf16[16,8,256]{2,1,0:T(8,128)(2,1)S(1)} %get-tuple-element.52), channel_id=1, replica_groups=mesh['lat'=16,'mem'=16] {'mem'}, dimensions={0} | all-to-all | bytes 131072 | tf_op jit(solution)/shard_map/all_to_all | solution.py:309
  58.7 3.6 %all-to-all-start.1 = ((bf16[16,96,256]{2,1,0:T(8,128)(2,1)}), bf16[16,96,256]{2,1,0:T(8,128)(2,1)S(1)}, u32[]{:S(2)}, u32[]{:S(2)}) async-start(bf16[16,96,256]{2,1,0:T(8,128)(2,1)} %get-tuple-element.54), calls=%async_computation.1 | async-start | bytes 1572864 | tf_op jit(solution)/shard_map/all_to_all | solution.py:311
  62.3 0.0 copy-done.5
  62.3 0.0 copy-done.6
  62.3 0.8 shard_map.98
  63.1 7.0 %collective-permute-start.10 = (f32[32,128]{1,0:T(8,128)S(1)}, f32[32,128]{1,0:T(8,128)S(1)}, u32[]{:S(2)}, u32[]{:S(2)}) collective-permute-start(f32[32,128]{1,0:T(8,128)S(1)} %shard_map.98), channel_id=1, source_target_pairs={{0,48},{16,32},{32,16},{48,0},{64,112},{80,96},{96,80},{112,64},{1... | collective-permute-start | bytes 49160 | tf_op jit(solution)/shard_map/ppermute | solution.py:315
  70.2 0.0 collective-permute-start.8
  70.2 1.3 %collective-permute-start.9 = (f32[32,128]{1,0:T(8,128)S(1)}, f32[32,128]{1,0:T(8,128)S(1)}, u32[]{:S(2)}, u32[]{:S(2)}) collective-permute-start(f32[32,128]{1,0:T(8,128)S(1)} %shard_map.98), channel_id=1, source_target_pairs={{0,32},{16,48},{32,0},{48,16},{64,96},{80,112},{96,64},{112,80},{1... | collective-permute-start | bytes 49160 | tf_op jit(solution)/shard_map/ppermute | solution.py:315
  71.4 0.2 collective-permute-done.10
  71.6 1.5 %collective-permute-done.8 = f32[32,128]{1,0:T(8,128)S(1)} collective-permute-done((f32[32,128]{1,0:T(8,128)S(1)}, f32[32,128]{1,0:T(8,128)S(1)}, u32[]{:S(2)}, u32[]{:S(2)}) %collective-permute-start.8) | collective-permute-done | bytes 16416 | tf_op jit(solution)/shard_map/ppermute | solution.py:315
  73.0 1.5 %collective-permute-done.9 = f32[32,128]{1,0:T(8,128)S(1)} collective-permute-done((f32[32,128]{1,0:T(8,128)S(1)}, f32[32,128]{1,0:T(8,128)S(1)}, u32[]{:S(2)}, u32[]{:S(2)}) %collective-permute-start.9) | collective-permute-done | bytes 16416 | tf_op jit(solution)/shard_map/ppermute | solution.py:315
  74.6 1.2 %collective-permute-start.11 = (f32[32,128]{1,0:T(8,128)S(1)}, f32[32,128]{1,0:T(8,128)S(1)}, u32[]{:S(2)}, u32[]{:S(2)}) collective-permute-start(f32[32,128]{1,0:T(8,128)S(1)} %add_add_fusion.a_ref), channel_id=1, source_target_pairs={{0,64},{16,80},{32,96},{48,112},{64,0},{80,16},{96,32},{112,48},{1... | collective-permute-start | bytes 49160 | tf_op jit(solution)/shard_map/ppermute | solution.py:315
  75.8 1.6 %collective-permute-start.12 = (f32[32,128]{1,0:T(8,128)S(1)}, f32[32,128]{1,0:T(8,128)S(1)}, u32[]{:S(2)}, u32[]{:S(2)}) collective-permute-start(f32[32,128]{1,0:T(8,128)S(1)} %add_add_fusion.a_ref), channel_id=1, source_target_pairs={{0,128},{16,144},{32,160},{48,176},{64,192},{80,208},{96,224},{112... | collective-permute-start | bytes 49160 | tf_op jit(solution)/shard_map/ppermute | solution.py:315
  77.4 1.0 collective-permute-start.13
  78.4 0.0 collective-permute-done.11.b_ref
  78.4 1.4 %collective-permute-done.12.c_ref = f32[32,128]{1,0:T(8,128)S(1)} collective-permute-done((f32[32,128]{1,0:T(8,128)S(1)}, f32[32,128]{1,0:T(8,128)S(1)}, u32[]{:S(2)}, u32[]{:S(2)}) %collective-permute-start.12) | collective-permute-done | bytes 16416 | tf_op jit(solution)/shard_map/ppermute | solution.py:315
  79.9 1.6 %collective-permute-done.13.d_ref = f32[32,128]{1,0:T(8,128)S(1)} collective-permute-done((f32[32,128]{1,0:T(8,128)S(1)}, f32[32,128]{1,0:T(8,128)S(1)}, u32[]{:S(2)}, u32[]{:S(2)}) %collective-permute-start.13) | collective-permute-done | bytes 16416 | tf_op jit(solution)/shard_map/ppermute | solution.py:315
  81.5 2.5 %shard_map.99.weight_ref = bf16[32,32]{1,0:T(8,128)(2,1)S(1)} custom-call(f32[32,128]{1,0:T(8,128)S(1)} %add_add_fusion.a_ref, f32[32,128]{1,0:T(8,128)S(1)} %collective-permute-done.11.b_ref, f32[32,128]{1,0:T(8,128)S(1)} %collective-permute-done.12.c_ref, f32[32,128]{1,0:T(8,128)S(1)} %collective-permute-done.13.d_ref), custom_call_target="tpu_custom_call" | custom-call | tf_op jit(solution)/shard_map/pallas_call | solution.py:22
  84.0 1.0 all-to-all-done.1.share_ref
  85.0 0.8 shard_map.100
  85.8 31.5 %all_to_all.16.in_ref = bf16[16,2,48,256]{3,2,1,0:T(8,128)(2,1)S(1)} all-to-all(bf16[16,2,48,256]{3,2,1,0:T(8,128)(2,1)S(1)} %bitcast.4), channel_id=1, replica_groups=mesh['lat'=16,'mem'=16] {'mem'}, dimensions={0} | all-to-all | bytes 1572864 | tf_op jit(solution)/shard_map/all_to_all | solution.py:327
  117.3 1.1 shard_map.101
  (3 shorter events, 0.0 us)
Async XLA Ops:
  0.0 0.7 copy-start.2
  2.1 11.1 %collective-permute-start.4 = (bf16[720,256]{1,0:T(8,128)(2,1)S(1)}, bf16[720,256]{1,0:T(8,128)(2,1)S(1)}, u32[]{:S(2)}, u32[]{:S(2)}) collective-permute-start(bf16[720,256]{1,0:T(8,128)(2,1)S(1)} %get-tuple-element.45.mid_ref), channel_id=1, source_target_pairs={{0,16},{32,48},{64,80},{96,112},{128,144},{160,176},{192,208},{224... | collective-permute-start | bytes 1105928 | tf_op jit(solution)/shard_map/ppermute | solution.py:252
  4.3 8.9 %collective-permute-start.5 = (bf16[720,256]{1,0:T(8,128)(2,1)S(1)}, bf16[720,256]{1,0:T(8,128)(2,1)S(1)}, u32[]{:S(2)}, u32[]{:S(2)}) collective-permute-start(bf16[720,256]{1,0:T(8,128)(2,1)S(1)} %get-tuple-element.45.mid_ref), channel_id=1, source_target_pairs={{16,32},{48,64},{80,96},{112,128},{144,160},{176,192},{208,224},{3... | collective-permute-start | bytes 1105928 | tf_op jit(solution)/shard_map/ppermute | solution.py:252
  5.0 15.4 %collective-permute-start = (bf16[720,256]{1,0:T(8,128)(2,1)S(1)}, bf16[720,256]{1,0:T(8,128)(2,1)S(1)}, u32[]{:S(2)}, u32[]{:S(2)}) collective-permute-start(bf16[720,256]{1,0:T(8,128)(2,1)S(1)} %get-tuple-element.31.mid_ref), channel_id=1, source_target_pairs={{0,16},{32,48},{64,80},{96,112},{128,144},{160,176},{192,208},{224... | collective-permute-start | bytes 1105928 | tf_op jit(solution)/shard_map/ppermute | solution.py:252
  8.6 11.8 %collective-permute-start.1 = (bf16[720,256]{1,0:T(8,128)(2,1)S(1)}, bf16[720,256]{1,0:T(8,128)(2,1)S(1)}, u32[]{:S(2)}, u32[]{:S(2)}) collective-permute-start(bf16[720,256]{1,0:T(8,128)(2,1)S(1)} %get-tuple-element.31.mid_ref), channel_id=1, source_target_pairs={{16,32},{48,64},{80,96},{112,128},{144,160},{176,192},{208,224},{3... | collective-permute-start | bytes 1105928 | tf_op jit(solution)/shard_map/ppermute | solution.py:252
  9.3 1.2 %copy-start = (bf16[2,256,1024]{2,1,0:T(8,128)(2,1)S(1)}, bf16[2,256,1024]{2,1,0:T(8,128)(2,1)}, u32[]{:S(2)}) copy-start(bf16[2,256,1024]{2,1,0:T(8,128)(2,1)} %refs_1_.2) | copy-start | bytes 3145732
  10.5 1.2 %copy-start.1 = (bf16[2,1024,256]{2,1,0:T(8,128)(2,1)S(1)}, bf16[2,1024,256]{2,1,0:T(8,128)(2,1)}, u32[]{:S(2)}) copy-start(bf16[2,1024,256]{2,1,0:T(8,128)(2,1)} %refs_2_.2) | copy-start | bytes 3145732
  16.2 14.5 %collective-permute-start.6 = (bf16[720,256]{1,0:T(8,128)(2,1)S(1)}, bf16[720,256]{1,0:T(8,128)(2,1)S(1)}, u32[]{:S(2)}, u32[]{:S(2)}) collective-permute-start(bf16[720,256]{1,0:T(8,128)(2,1)S(1)} %get-tuple-element.48.mid_ref), channel_id=1, source_target_pairs={{0,16},{32,48},{64,80},{96,112},{128,144},{160,176},{192,208},{224... | collective-permute-start | bytes 1105928 | tf_op jit(solution)/shard_map/ppermute | solution.py:252
  19.7 11.0 %collective-permute-start.7 = (bf16[720,256]{1,0:T(8,128)(2,1)S(1)}, bf16[720,256]{1,0:T(8,128)(2,1)S(1)}, u32[]{:S(2)}, u32[]{:S(2)}) collective-permute-start(bf16[720,256]{1,0:T(8,128)(2,1)S(1)} %get-tuple-element.48.mid_ref), channel_id=1, source_target_pairs={{16,32},{48,64},{80,96},{112,128},{144,160},{176,192},{208,224},{3... | collective-permute-start | bytes 1105928 | tf_op jit(solution)/shard_map/ppermute | solution.py:252
  23.4 10.7 %collective-permute-start.2 = (bf16[720,256]{1,0:T(8,128)(2,1)S(1)}, bf16[720,256]{1,0:T(8,128)(2,1)S(1)}, u32[]{:S(2)}, u32[]{:S(2)}) collective-permute-start(bf16[720,256]{1,0:T(8,128)(2,1)S(1)} %get-tuple-element.37.mid_ref), channel_id=1, source_target_pairs={{0,16},{32,48},{64,80},{96,112},{128,144},{160,176},{192,208},{224... | collective-permute-start | bytes 1105928 | tf_op jit(solution)/shard_map/ppermute | solution.py:252
  28.3 5.8 %collective-permute-start.3 = (bf16[720,256]{1,0:T(8,128)(2,1)S(1)}, bf16[720,256]{1,0:T(8,128)(2,1)S(1)}, u32[]{:S(2)}, u32[]{:S(2)}) collective-permute-start(bf16[720,256]{1,0:T(8,128)(2,1)S(1)} %get-tuple-element.37.mid_ref), channel_id=1, source_target_pairs={{16,32},{48,64},{80,96},{112,128},{144,160},{176,192},{208,224},{3... | collective-permute-start | bytes 1105928 | tf_op jit(solution)/shard_map/ppermute | solution.py:252
  29.2 1.5 %copy-start.3 = (s32[1024]{0:T(1024)S(1)}, s32[1024]{0:T(1024)}, u32[]{:S(2)}) copy-start(s32[1024]{0:T(1024)} %param.14) | copy-start | bytes 12292
  29.2 1.5 %copy-start.4 = (s32[1024]{0:T(1024)S(1)}, s32[1024]{0:T(1024)}, u32[]{:S(2)}) copy-start(s32[1024]{0:T(1024)} %param.15) | copy-start | bytes 12292
  38.3 23.9 %copy-start.5 = (f32[1024]{0:T(1024)S(1)}, f32[1024]{0:T(1024)}, u32[]{:S(2)}) copy-start(f32[1024]{0:T(1024)} %param.16) | copy-start | bytes 12292
  38.3 24.0 %copy-start.6 = (f32[1024]{0:T(1024)S(1)}, f32[1024]{0:T(1024)}, u32[]{:S(2)}) copy-start(f32[1024]{0:T(1024)} %param.17) | copy-start | bytes 12292
  58.7 26.3 %all-to-all-start.1 = ((bf16[16,96,256]{2,1,0:T(8,128)(2,1)}), bf16[16,96,256]{2,1,0:T(8,128)(2,1)S(1)}, u32[]{:S(2)}, u32[]{:S(2)}) async-start(bf16[16,96,256]{2,1,0:T(8,128)(2,1)} %get-tuple-element.54), calls=%async_computation.1 | async-start | bytes 1572864 | tf_op jit(solution)/shard_map/all_to_all | solution.py:311
  63.1 8.5 %collective-permute-start.10 = (f32[32,128]{1,0:T(8,128)S(1)}, f32[32,128]{1,0:T(8,128)S(1)}, u32[]{:S(2)}, u32[]{:S(2)}) collective-permute-start(f32[32,128]{1,0:T(8,128)S(1)} %shard_map.98), channel_id=1, source_target_pairs={{0,48},{16,32},{32,16},{48,0},{64,112},{80,96},{96,80},{112,64},{1... | collective-permute-start | bytes 49160 | tf_op jit(solution)/shard_map/ppermute | solution.py:315
  70.2 2.9 %collective-permute-start.8 = (f32[32,128]{1,0:T(8,128)S(1)}, f32[32,128]{1,0:T(8,128)S(1)}, u32[]{:S(2)}, u32[]{:S(2)}) collective-permute-start(f32[32,128]{1,0:T(8,128)S(1)} %shard_map.98), channel_id=1, source_target_pairs={{0,16},{16,0},{32,48},{48,32},{64,80},{80,64},{96,112},{112,96},{1... | collective-permute-start | bytes 49160 | tf_op jit(solution)/shard_map/ppermute | solution.py:315
  70.2 4.4 %collective-permute-start.9 = (f32[32,128]{1,0:T(8,128)S(1)}, f32[32,128]{1,0:T(8,128)S(1)}, u32[]{:S(2)}, u32[]{:S(2)}) collective-permute-start(f32[32,128]{1,0:T(8,128)S(1)} %shard_map.98), channel_id=1, source_target_pairs={{0,32},{16,48},{32,0},{48,16},{64,96},{80,112},{96,64},{112,80},{1... | collective-permute-start | bytes 49160 | tf_op jit(solution)/shard_map/ppermute | solution.py:315
  74.6 3.9 %collective-permute-start.11 = (f32[32,128]{1,0:T(8,128)S(1)}, f32[32,128]{1,0:T(8,128)S(1)}, u32[]{:S(2)}, u32[]{:S(2)}) collective-permute-start(f32[32,128]{1,0:T(8,128)S(1)} %add_add_fusion.a_ref), channel_id=1, source_target_pairs={{0,64},{16,80},{32,96},{48,112},{64,0},{80,16},{96,32},{112,48},{1... | collective-permute-start | bytes 49160 | tf_op jit(solution)/shard_map/ppermute | solution.py:315
  75.8 4.1 %collective-permute-start.12 = (f32[32,128]{1,0:T(8,128)S(1)}, f32[32,128]{1,0:T(8,128)S(1)}, u32[]{:S(2)}, u32[]{:S(2)}) collective-permute-start(f32[32,128]{1,0:T(8,128)S(1)} %add_add_fusion.a_ref), channel_id=1, source_target_pairs={{0,128},{16,144},{32,160},{48,176},{64,192},{80,208},{96,224},{112... | collective-permute-start | bytes 49160 | tf_op jit(solution)/shard_map/ppermute | solution.py:315
  77.4 4.1 %collective-permute-start.13 = (f32[32,128]{1,0:T(8,128)S(1)}, f32[32,128]{1,0:T(8,128)S(1)}, u32[]{:S(2)}, u32[]{:S(2)}) collective-permute-start(f32[32,128]{1,0:T(8,128)S(1)} %add_add_fusion.a_ref), channel_id=1, source_target_pairs={{0,192},{16,208},{32,224},{48,240},{64,128},{80,144},{96,160},{112... | collective-permute-start | bytes 49160 | tf_op jit(solution)/shard_map/ppermute | solution.py:315
